TPU v7x, 32 devices: a whole 2x2x4 slice. The times are simulated.
32 devices in a mesh: dp: 16 (over z, x, core), tensor: 2 (over y).
Axes of the slice: x: 2, y: 2, z: 4, core: 2. Of those that a mesh axis runs over, the one named last changes fastest.
Arguments:
- hidden_in: bfloat16 [16384, 1024], P(('dp', 'tensor')), may hold values from -6 to 6
- positions: int32 [16384], P('dp'), may hold values from 0 to 1023, as said below
- gain_attention: float32 [1024], replicated, may hold values from 0.1 to 1.9
- gain_feedforward: float32 [1024], replicated, may hold values from 0.1 to 1.9
- gain_query: float32 [128], replicated, may hold values from 0.7 to 5
- gain_key: float32 [128], replicated, may hold values from 0.7 to 5
- query_proj: bfloat16 [1024, 2048], P('dp', 'tensor'), may hold values from -0.1875 to 0.1875
- key_proj: bfloat16 [1024, 1024], P('dp', 'tensor'), may hold values from -0.1875 to 0.1875
- value_proj: bfloat16 [1024, 1024], P('dp', 'tensor'), may hold values from -0.1875 to 0.1875
- out_proj: bfloat16 [2048, 1024], P(('tensor', 'dp')), may hold values from -3 to 3
- gate_proj: bfloat16 [1024, 3072], P('dp', 'tensor'), may hold values from -0.1875 to 0.1875
- up_proj: bfloat16 [1024, 3072], P('dp', 'tensor'), may hold values from -0.1875 to 0.1875
- down_proj: bfloat16 [3072, 1024], P(('tensor', 'dp')), may hold values from -0.21875 to 0.21875
- cotangent: bfloat16 [16384, 1024], P(('dp', 'tensor')), may hold values from -6 to 6
Outputs:
- hidden_out: bfloat16 [16384, 1024], P(('dp', 'tensor'))
- grad_hidden: float32 [16384, 1024], P(('dp', 'tensor'))
- attention_gain_grad: float32 [1024], replicated
- feedforward_gain_grad: float32 [1024], replicated
- query_gain_grad: float32 [128], replicated
- key_gain_grad: float32 [128], replicated
- query_grads: float32 [1024, 2048], P('dp', 'tensor')
- key_grads: float32 [1024, 1024], P('dp', 'tensor')
- value_grads: float32 [1024, 1024], P('dp', 'tensor')
- out_grads: float32 [2048, 1024], P(('tensor', 'dp'))
- gate_grads: float32 [1024, 3072], P('dp', 'tensor')
- up_grads: float32 [1024, 3072], P('dp', 'tensor')
- down_grads: float32 [3072, 1024], P(('tensor', 'dp'))
Inputs may be any that keep to these rules, and one draw needn't show every extreme that they name: Within each sequence of 1024 tokens the positions start at 0 and rise by one from token to token, except that they restart at 0 where a document begins; some sequence holds one document.
All inputs are finite; a program needn't handle non-finite values.
Results may differ from a plain program's by a relative error of at most 0.02.
The roundings to bfloat16 on the way count: a program that leaves them out, or rounds other values in their place, can miss the bound.
Values may be sent and summed in bfloat16 or wider, within the bound.
No kernel may reach another device: no remote copies, remote signals or barrier semaphores. Data moves between devices by JAX's collectives and lax.ppermute only.
A program may use at most 256 MiB of HBM per device.

v0:
```python
import math
import jax
import jax.numpy as jnp
from jax import lax
from jax.sharding import PartitionSpec as P

HD = 128
EPS = 1e-06
THETA = 1000000.0
BF = jnp.bfloat16
F32 = jnp.float32


def rotary_tables(positions, width):
    half_width = width // 2
    freq_index = jnp.arange(half_width).astype(F32)
    inverse_freq = jnp.exp(freq_index * (-2.0 * math.log(THETA) / width))
    angles = positions.astype(F32)[:, None] * inverse_freq[None, :]
    return (jnp.cos(angles)[:, None, :], jnp.sin(angles)[:, None, :])


def rotate(values, cosine_table, sine_table):
    half_width = values.shape[-1] // 2
    lower_half = values[..., :half_width]
    upper_half = values[..., half_width:]
    return jnp.concatenate(
        (
            lower_half * cosine_table - upper_half * sine_table,
            upper_half * cosine_table + lower_half * sine_table,
        ),
        -1,
    )


def rms_unit(values):
    inv_scale = lax.rsqrt(jnp.mean(values * values, -1, keepdims=True) + EPS)
    return (values * inv_scale, inv_scale)


def rms_back(grad_out, gain_vec, unit_vals, inv_scale):
    scaled_grad = grad_out * gain_vec
    return inv_scale * (
        scaled_grad - unit_vals * jnp.mean(scaled_grad * unit_vals, -1, keepdims=True)
    )


def matmul(left, right):
    return jnp.dot(left, right, preferred_element_type=F32)


def contract_rows(left, right):
    return lax.dot_general(left, right, (((0,), (0,)), ((), ())), preferred_element_type=F32)


def contract_cols(left, right):
    return lax.dot_general(left, right, (((1,), (1,)), ((), ())), preferred_element_type=F32)


def attend(query_b, key_b, value_b):
    length = query_b.shape[0]
    block_rows = min(length, 512)
    block_count = length // block_rows
    scale_qk = 1.0 / math.sqrt(query_b.shape[-1])
    outputs = []
    log_sums = []
    for block in range(block_count):
        row_start = block * block_rows
        key_end = row_start + block_rows
        query_block = query_b[row_start:key_end]
        scores = (
            jnp.einsum("qgrd,kgd->grqk", query_block, key_b[:key_end], preferred_element_type=F32)
            * scale_qk
        )
        causal = (row_start + jnp.arange(block_rows, dtype=jnp.int32))[:, None] >= jnp.arange(
            key_end, dtype=jnp.int32
        )[None, :]
        scores = jnp.where(causal, scores, -jnp.inf)
        top_score = jnp.max(scores, -1, keepdims=True)
        shifted = jnp.exp(scores - top_score)
        sum_exp = jnp.sum(shifted, -1, keepdims=True)
        probs_b = (shifted / sum_exp).astype(BF)
        outputs.append(
            jnp.einsum("grqk,kgd->qgrd", probs_b, value_b[:key_end], preferred_element_type=F32)
        )
        log_sums.append(top_score + jnp.log(sum_exp))
    return (jnp.concatenate(outputs, 0), log_sums)


def attend_back(query_b, key_b, value_b, grad_b, log_sums):
    length = query_b.shape[0]
    block_rows = min(length, 512)
    block_count = length // block_rows
    scale_qk = 1.0 / math.sqrt(query_b.shape[-1])
    key_acc = jnp.zeros(key_b.shape, F32)
    value_acc = jnp.zeros(key_b.shape, F32)
    grad_queries = []
    for block in range(block_count):
        row_start = block * block_rows
        key_end = row_start + block_rows
        query_block = query_b[row_start:key_end]
        grad_block = grad_b[row_start:key_end]
        keys_seen = key_b[:key_end]
        scores = (
            jnp.einsum("qgrd,kgd->grqk", query_block, keys_seen, preferred_element_type=F32)
            * scale_qk
        )
        causal = (row_start + jnp.arange(block_rows, dtype=jnp.int32))[:, None] >= jnp.arange(
            key_end, dtype=jnp.int32
        )[None, :]
        scores = jnp.where(causal, scores, -jnp.inf)
        probs = jnp.exp(scores - log_sums[block])
        probs_b = probs.astype(BF)
        grad_probs = jnp.einsum(
            "qgrd,kgd->grqk", grad_block, value_b[:key_end], preferred_element_type=F32
        )
        row_dot = jnp.sum(probs * grad_probs, -1, keepdims=True)
        grad_scores_b = (probs * (grad_probs - row_dot)).astype(BF)
        grad_queries.append(
            jnp.einsum("grqk,kgd->qgrd", grad_scores_b, keys_seen, preferred_element_type=F32)
            * scale_qk
        )
        key_acc = key_acc.at[:key_end].add(
            jnp.einsum("grqk,qgrd->kgd", grad_scores_b, query_block, preferred_element_type=F32)
            * scale_qk
        )
        value_acc = value_acc.at[:key_end].add(
            jnp.einsum("grqk,qgrd->kgd", probs_b, grad_block, preferred_element_type=F32)
        )
    return (jnp.concatenate(grad_queries, 0), key_acc, value_acc)


def all_sum(value, sizes):
    for axis, size in sizes:
        if size & size - 1:
            value = lax.psum(value, axis)
            continue
        step = 1
        while step < size:
            value = value + lax.ppermute(value, axis, [(i, i ^ step) for i in range(size)])
            step *= 2
    return value


def make_local(n_dp, n_tensor):
    paired = n_tensor == 2
    swap = [(0, 1), (1, 0)]

    def gather_rows(own):
        if paired:
            return jnp.concatenate((own, lax.ppermute(own, "tensor", swap)), 0)
        return lax.all_gather(own, "tensor", axis=0, tiled=True)

    def to_sequence(rows):
        if not paired:
            return rows
        half = rows.shape[0] // 2
        first = lax.axis_index("tensor") == 0
        return jnp.concatenate(
            (
                jnp.where(first, rows[:half], rows[half:]),
                jnp.where(first, rows[half:], rows[:half]),
            ),
            0,
        )

    def scatter_rows(part, operand):
        if paired:
            half = operand[0].shape[0] // 2
            sent = part(*(o[half:] for o in operand)).astype(BF)
            got = lax.ppermute(sent, "tensor", swap)
            return part(*(o[:half] for o in operand)) + got.astype(F32)
        return lax.psum_scatter(
            part(*operand).astype(BF), "tensor", scatter_dimension=0, tiled=True
        ).astype(F32)

    def local(
        hidden_in,
        positions,
        gain_attention,
        gain_feedforward,
        gain_query,
        gain_key,
        query_proj,
        key_proj,
        value_proj,
        out_proj,
        gate_proj,
        up_proj,
        down_proj,
        cotangent,
    ):
        length = positions.shape[0]
        own = hidden_in.shape[0]
        width = hidden_in.shape[1]
        heads_here = query_proj.shape[1] // HD
        groups_here = key_proj.shape[1] // HD
        width_query = heads_here * HD
        width_key = groups_here * HD
        width_qkv = width_query + 2 * width_key
        units = gate_proj.shape[1]
        shard_rows = query_proj.shape[0]
        shard_attn = jnp.concatenate(
            (query_proj, key_proj, value_proj, out_proj.reshape(shard_rows, -1)), 1
        )
        shard_mlp = jnp.concatenate((gate_proj, up_proj, down_proj.reshape(shard_rows, -1)), 1)
        full_attn = lax.all_gather(shard_attn, "dp", axis=0, tiled=True)
        full_mlp = lax.all_gather(shard_mlp, "dp", axis=0, tiled=True)
        proj_qkv = full_attn[:, :width_qkv]
        full_out = full_attn[:, width_qkv:].reshape(-1, width)
        full_gateup = full_mlp[:, : 2 * units]
        full_down = full_mlp[:, 2 * units :].reshape(-1, width)
        rows_hidden = gather_rows(hidden_in)
        rows_cot = gather_rows(cotangent)
        cosine_table, sine_table = rotary_tables(positions, HD)
        unit_rows, scale_rows = rms_unit(rows_hidden.astype(F32))
        rows_attn = (unit_rows * gain_attention).astype(BF)
        if paired:
            hidden_f, unit_attn, scale_attn = (
                hidden_in.astype(F32),
                unit_rows[:own],
                scale_rows[:own],
            )
        else:
            hidden_f = hidden_in.astype(F32)
            unit_attn, scale_attn = rms_unit(hidden_f)
        projected = to_sequence(matmul(rows_attn, proj_qkv))
        query_raw = projected[:, :width_query].reshape(length, heads_here, HD)
        key_raw = projected[:, width_query : width_query + width_key].reshape(
            length, groups_here, HD
        )
        value_b = (
            projected[:, width_query + width_key :].astype(BF).reshape(length, groups_here, HD)
        )
        query_unit, query_scale = rms_unit(query_raw)
        key_unit, key_scale = rms_unit(key_raw)
        query_b = (
            rotate(query_unit * gain_query, cosine_table, sine_table)
            .astype(BF)
            .reshape(length, groups_here, heads_here // groups_here, HD)
        )
        key_b = rotate(key_unit * gain_key, cosine_table, sine_table).astype(BF)
        heads_out, log_sums = attend(query_b, key_b, value_b)
        heads_b = to_sequence(heads_out.reshape(length, width_query).astype(BF))
        resid = hidden_f + scatter_rows(lambda h: matmul(h, full_out), (heads_b,))
        unit_mlp, scale_mlp = rms_unit(resid)
        rows_mlp = gather_rows((unit_mlp * gain_feedforward).astype(BF))
        gate_val = matmul(rows_mlp, full_gateup[:, :units])
        up_val = matmul(rows_mlp, full_gateup[:, units:])
        sigmoid_gate = jax.nn.sigmoid(gate_val)
        active_b = (gate_val * sigmoid_gate * up_val).astype(BF)
        output_b = (resid + scatter_rows(lambda a: matmul(a, full_down), (active_b,))).astype(BF)
        grad_active = contract_cols(rows_cot, full_down)
        grad_gate_b = (
            grad_active * up_val * sigmoid_gate * (1.0 + gate_val * (1.0 - sigmoid_gate))
        ).astype(BF)
        grad_up_b = (grad_active * gate_val * sigmoid_gate).astype(BF)
        grad_normed_mlp = scatter_rows(
            lambda g, u: contract_cols(g, full_gateup[:, :units])
            + contract_cols(u, full_gateup[:, units:]),
            (grad_gate_b, grad_up_b),
        )
        grad_mlp_w = jnp.concatenate(
            (
                contract_rows(rows_mlp, grad_gate_b).astype(BF),
                contract_rows(rows_mlp, grad_up_b).astype(BF),
                contract_rows(active_b, rows_cot).astype(BF).reshape(width, -1),
            ),
            1,
        )
        sent_mlp = lax.psum_scatter(grad_mlp_w, "dp", scatter_dimension=0, tiled=True)
        term_feedforward = jnp.sum(grad_normed_mlp * unit_mlp, 0)
        grad_resid = cotangent.astype(F32) + rms_back(
            grad_normed_mlp, gain_feedforward, unit_mlp, scale_mlp
        )
        rows_resid = gather_rows(grad_resid.astype(BF))
        grad_heads_b = to_sequence(contract_cols(rows_resid, full_out).astype(BF)).reshape(
            length, groups_here, heads_here // groups_here, HD
        )
        grad_qrot, grad_krot, grad_value = attend_back(
            query_b, key_b, value_b, grad_heads_b, log_sums
        )
        grad_qnormed = rotate(grad_qrot.reshape(length, heads_here, HD), cosine_table, -sine_table)
        grad_knormed = rotate(grad_krot, cosine_table, -sine_table)
        term_query = jnp.sum(grad_qnormed * query_unit, (0, 1))
        term_key = jnp.sum(grad_knormed * key_unit, (0, 1))
        grad_qkv_b = to_sequence(
            jnp.concatenate(
                (
                    rms_back(grad_qnormed, gain_query, query_unit, query_scale).reshape(
                        length, width_query
                    ),
                    rms_back(grad_knormed, gain_key, key_unit, key_scale).reshape(
                        length, width_key
                    ),
                    grad_value.reshape(length, width_key),
                ),
                1,
            ).astype(BF)
        )
        grad_attn_w = jnp.concatenate(
            (
                contract_rows(rows_attn, grad_qkv_b).astype(BF),
                contract_rows(heads_b, rows_resid).astype(BF).reshape(width, -1),
            ),
            1,
        )
        sent_attn = lax.psum_scatter(grad_attn_w, "dp", scatter_dimension=0, tiled=True)
        grad_normed_attn = scatter_rows(lambda g: contract_cols(g, proj_qkv), (grad_qkv_b,))
        term_attention = jnp.sum(grad_normed_attn * unit_attn, 0)
        grad_hidden = grad_resid + rms_back(grad_normed_attn, gain_attention, unit_attn, scale_attn)
        terms = all_sum(
            jnp.concatenate((term_attention, term_feedforward, term_query, term_key)).reshape(
                -1, HD
            ),
            (("tensor", n_tensor), ("dp", n_dp)),
        ).reshape(-1)
        sent_attn = sent_attn.astype(F32)
        sent_mlp = sent_mlp.astype(F32)
        return (
            output_b,
            grad_hidden,
            terms[:width],
            terms[width : 2 * width],
            terms[2 * width : 2 * width + HD],
            terms[2 * width + HD :],
            sent_attn[:, :width_query],
            sent_attn[:, width_query : width_query + width_key],
            sent_attn[:, width_query + width_key : width_qkv],
            sent_attn[:, width_qkv:].reshape(out_proj.shape),
            sent_mlp[:, :units],
            sent_mlp[:, units : 2 * units],
            sent_mlp[:, 2 * units :].reshape(down_proj.shape),
        )

    return local


def solution(mesh):
    rows = P(("dp", "tensor"), None)
    cut = P("dp", "tensor")
    stacked = P(("tensor", "dp"), None)
    return jax.shard_map(
        make_local(mesh.shape["dp"], mesh.shape["tensor"]),
        mesh=mesh,
        in_specs=(
            rows,
            P("dp"),
            P(),
            P(),
            P(),
            P(),
            cut,
            cut,
            cut,
            stacked,
            cut,
            cut,
            stacked,
            rows,
        ),
        out_specs=(rows, rows, P(), P(), P(), P(), cut, cut, cut, stacked, cut, cut, stacked),
        check_vma=False,
    )
```

profile of v0, /device:TPU:0, one launch (start us, length us, event | category | flops | bytes accessed | tf_op | source)
XLA Modules:
  0.0 633.6 jit_solution(4155793221985874017)
XLA Ops:
  12.2 3.1 collective-permute-start
  17.3 2.9 fusion.117
  20.3 18.2 %collective-permute-done = bf16[512,1024]{1,0:T(8,128)(2,1)S(1)} collective-permute-done((bf16[512,1024]{1,0:T(8,128)(2,1)S(1)}, bf16[512,1024]{1,0:T(8,128)(2,1)S(1)}, u32[]{:S(2)}, u32[]{:S(2)}) %collective-permute-start) | collective-permute-done | bytes 1048608 | tf_op jit(solution)/shard_map/ppermute | solution.py:150
  39.0 36.1 %all-gather.3.cloned.1.call-done = bf16[1024,3072]{1,0:T(8,128)(2,1)} async-done(((bf16[64,3072]{1,0:T(8,128)(2,1)}), bf16[1024,3072]{1,0:T(8,128)(2,1)}) %all-gather.3.cloned.1.call-update) | async-done | bytes 6291472 | tf_op jit(solution)/shard_map/all_gather | solution.py:206
  75.0 10.0 %fusion.36 = f32[1024,2048]{1,0:T(8,128)} fusion(bf16[1024,3072]{1,0:T(8,128)(2,1)} %all-gather.3.cloned.1.call-done, f32[1024]{0:T(1024)S(1)} %copy-done.74, f32[1024]{0:T(1024)S(1)} %add_rsqrt_fusion.2, bf16[512,1024]{1,0:T(8,128)(2,1)S(1)} %collective-permute-done, bf16[512,1024]{1,0:T(8,128)(2,1)S(1)} %copy-done.40), kind=kOutput, calls=%fused_computation.77 | convolution fusion | flops 4302307328 | bytes 14688256 | tf_op jit(solution)/shard_map/dot_general | solution.py:48
  85.0 4.3 slice_select_fusion.1
  89.4 3.3 fusion.5
  92.7 2.2 slice.327
  97.5 2.4 multiply_multiply_fusion
  105.1 2.2 reshape.385
  107.3 3.7 multiply_reduce_fusion.8
  112.3 2.4 copy.156
  123.5 2.2 copy-done
  125.7 7.5 %fusion.135 = (f32[4,2,512]{2,1,0:T(2,128)S(1)}, f32[4,2,512,1024]{2,3,1,0:T(8,128)}) fusion(bf16[512,4,2,128]{3,0,2,1:T(8,128)(2,1)S(1)} %bitcast.234, bf16[1024,4,64]{2,0,1:T(8,128)(2,1)S(1)} %get-tuple-element.107, bf16[1024,4,64]{2,0,1:T(8,128)(2,1)S(1)} %get-tuple-element.106, pred[512,1024]{0,1:T(8,128)(4,1)S(1)} %copy-done.58), kind=kOutput, calls=%fused_computation.226 | convolution fusion | flops 1088417792 | bytes 19415040 | tf_op jit(solution)/shard_map/qgrd,kgd->grqk/dot_general | solution.py:71
  133.2 8.3 %fusion.3 = f32[4,2,512]{2,1,0:T(2,128)S(1)} fusion(f32[4,2,512,1024]{2,3,1,0:T(8,128)} %get-tuple-element.129, f32[4,2,512]{2,1,0:T(2,128)S(1)} %get-tuple-element.128), kind=kLoop, calls=%fused_computation.9 | loop fusion | flops 8384512 | bytes 16809984 | tf_op jit(solution)/shard_map/reduce_sum | solution.py:80
  141.6 7.8 %fusion.80 = bf16[4,128,2,512]{3,1,2,0:T(8,128)(2,1)S(1)} fusion(f32[4,2,512,1024]{2,3,1,0:T(8,128)} %get-tuple-element.129, f32[4,2,512]{2,1,0:T(2,128)S(1)} %fusion.3, f32[4,2,512]{2,1,0:T(2,128)S(1)} %get-tuple-element.128, bf16[1024,4,128,1]{2,1,0,3:T(4,128)(2,1)S(1)} %bitcast.237), kind=kOutput, calls=%fused_computation.156 | convolution fusion | flops 1086849024 | bytes 18907136 | tf_op jit(solution)/shard_map/grqk,kgd->qgrd/dot_general | solution.py:83
  149.4 2.3 broadcast_select_fusion.3
  151.8 3.6 fusion.84
  157.6 24.0 %collective-permute-done.1 = bf16[512,1024]{1,0:T(8,128)(2,1)S(1)} collective-permute-done((bf16[512,1024]{1,0:T(8,128)(2,1)S(1)}, bf16[512,1024]{1,0:T(8,128)(2,1)S(1)}, u32[]{:S(2)}, u32[]{:S(2)}) %collective-permute-start.1) | collective-permute-done | bytes 1048608 | tf_op jit(solution)/shard_map/ppermute | solution.py:170
  181.6 3.2 multiply_reduce_fusion.7
  188.9 15.2 %collective-permute-done.4 = bf16[512,1024]{1,0:T(8,128)(2,1)S(1)} collective-permute-done((bf16[512,1024]{1,0:T(8,128)(2,1)S(1)}, bf16[512,1024]{1,0:T(8,128)(2,1)S(1)}, u32[]{:S(2)}, u32[]{:S(2)}) %collective-permute-start.4) | collective-permute-done | bytes 1048608 | tf_op jit(solution)/shard_map/ppermute | solution.py:150
  205.1 3.7 slice.345
  208.8 5.9 reshape.389
  214.7 8.8 %fusion.136 = f32[1024,1536]{1,0:T(8,128)} fusion(bf16[1024,1024]{1,0:T(8,128)(2,1)} %constant_dynamic-update-slice_fusion, bf16[1536,1024]{1,0:T(8,128)(2,1)} %reshape.389), kind=kOutput, calls=%fused_computation.227 | convolution fusion | flops 3221225472 | bytes 11534336 | tf_op jit(solution)/shard_map/dot_general | solution.py:56
  223.5 2.3 collective-permute-done.2
  225.9 8.6 %fusion.42 = f32[1024,1536]{1,0:T(8,128)} fusion(bf16[1024,4608]{1,0:T(8,128)(2,1)} %all-gather.5.cloned.1.call-done, bf16[512,1024]{1,0:T(8,128)(2,1)} %collective-permute-done.2, bf16[512,1024]{1,0:T(8,128)(2,1)} %multiply_convert_fusion.4), kind=kOutput, calls=%fused_computation.83 | convolution fusion | flops 3225419776 | bytes 11534336 | tf_op jit(solution)/shard_map/dot_general | solution.py:48
  234.5 10.6 %multiply_convert_fusion.1 = (bf16[1024,1536]{1,0:T(8,128)(2,1)S(1)}, bf16[1024,1536]{1,0:T(8,128)(2,1)}, bf16[1024,1536]{1,0:T(8,128)(2,1)S(1)}) fusion(f32[1024,1536]{1,0:T(8,128)} %fusion.136, f32[1024,1536]{1,0:T(8,128)} %fusion.42, bf16[1024,4608]{1,0:T(8,128)(2,1)S(1)} %bitcast.242, bf16[512,1024]{1,0:T(8,128)(2,1)} %collective-permute-done.2, ...), kind=kOutput, calls=%fused_computation.34 | convolution fusion | flops 3250585600 | bytes 27262976 | tf_op jit(solution)/shard_map/dot_general | solution.py:48
  252.2 21.1 %collective-permute-done.5 = bf16[512,1024]{1,0:T(8,128)(2,1)S(1)} collective-permute-done((bf16[512,1024]{1,0:T(8,128)(2,1)S(1)}, bf16[512,1024]{1,0:T(8,128)(2,1)S(1)}, u32[]{:S(2)}, u32[]{:S(2)}) %collective-permute-start.5) | collective-permute-done | bytes 1048608 | tf_op jit(solution)/shard_map/ppermute | solution.py:170
  273.3 2.8 multiply_reduce_fusion.2
  281.0 20.6 %collective-permute-done.6 = bf16[512,1024]{1,0:T(8,128)(2,1)S(1)} collective-permute-done((bf16[512,1024]{1,0:T(8,128)(2,1)}, bf16[512,1024]{1,0:T(8,128)(2,1)S(1)}, u32[]{:S(2)}, u32[]{:S(2)}) %collective-permute-start.6) | collective-permute-done | bytes 1048608 | tf_op jit(solution)/shard_map/ppermute | solution.py:150
  301.6 4.7 convolution_convert_fusion.3
  309.4 2.7 fusion.10
  312.1 2.4 multiply_bitcast_fusion.1
  314.5 2.2 fusion.104
  316.7 2.5 fusion.100
  319.2 11.2 %fusion = (f32[4,2,512]{2,1,0:T(2,128)}, f32[4,1024,512,2]{2,1,3,0:T(8,128)}) fusion(f32[4,2,512,1024]{2,3,1,0:T(8,128)S(1)} %bitcast.217, f32[4,2,512]{2,1,0:T(2,128)} %bitcast.246, bf16[512,4,2,128]{0,3,2,1:T(8,128)(2,1)} %bitcast.230, bf16[1024,4,128,1]{2,1,0,3:T(4,128)(2,1)} %bitcast.236), kind=kOutput, calls=%fused_computation.2 | convolution fusion | flops 1086320640 | bytes 35684352 | tf_op jit(solution)/shard_map/qgrd,kgd->grqk/dot_general | solution.py:113
  330.5 8.4 %fusion.2 = bf16[4,2,512,1024]{2,3,1,0:T(8,128)(2,1)S(1)} fusion(f32[4,1024,512,2]{2,1,3,0:T(8,128)} %get-tuple-element.136, f32[4,2,512,1024]{2,3,1,0:T(8,128)S(1)} %bitcast.217, f32[4,2,512]{2,1,0:T(2,128)} %get-tuple-element.135, f32[4,2,512]{2,1,0:T(2,128)} %bitcast.247), kind=kLoop, calls=%fused_computation.4 | loop fusion | flops 16777216 | bytes 41975808 | tf_op jit(solution)/shard_map/convert_element_type | solution.py:117
  344.5 3.9 copy.226
  348.4 2.7 copy.227
  351.2 4.1 multiply_subtract_fusion
  356.0 17.1 %multiply_reduce_fusion = (f32[1024,8]{1,0:T(8,128)S(1)}, f32[1024,8,128]{2,1,0:T(8,128)}) fusion(f32[1024,8,128]{2,1,0:T(8,128)S(1)} %bitcast.221, f32[128]{0:T(128)S(1)} %copy-done.71, f32[1024,8]{1,0:T(8,128)S(1)} %copy-done.27, f32[1024,8,64]{2,1,0:T(8,128)S(1)} %get-tuple-element.89, f32[1024,8,64]{2,1,0:T(8,128)S(1)} %get-tuple-element.88), kind=kLoop, calls=%fused_computation.57 | loop fusion | flops 5234688 | bytes 12648960 | tf_op jit(solution)/shard_map/reduce_sum | solution.py:43
  373.9 2.3 bitcast_add_fusion.1
  377.8 2.8 fusion.111
  381.7 9.9 %fusion.59 = bf16[1024,4,128]{0,2,1:T(8,128)(2,1)} fusion(f32[512,4,128]{0,2,1:T(8,128)} %fusion.100, bf16[512,4,2,128]{0,3,2,1:T(8,128)(2,1)S(1)} %bitcast.231, f32[4,2,512,1024]{2,3,1,0:T(8,128)} %get-tuple-element.129, f32[4,2,512]{2,1,0:T(2,128)S(1)} %bitcast.248), kind=kOutput, calls=%fused_computation.112 | convolution fusion | flops 1083179008 | bytes 19939328 | tf_op jit(solution)/shard_map/grqk,qgrd->kgd/dot_general | solution.py:127
  391.7 2.3 copy.225
  394.0 2.3 mul.521
  398.5 7.0 %fusion.22 = (f32[1024]{0:T(1024)S(1)}, bf16[1024,1024]{1,0:T(8,128)(2,1)S(1)}) fusion(f32[128,8,8,128]{3,2,1,0:T(8,128)} %bitcast.222, f32[128,8,8,128]{3,2,1,0:T(8,128)S(1)} %bitcast.225, f32[512,2048]{1,0:T(8,128)S(1)} %copy-done.4, f32[512,2048]{1,0:T(8,128)S(1)} %copy-done.2, f32[128,8,8,128]{3,2,1,0:T(8,128)S(1)} %bitcast.224, ...), kind=kLoop, calls=%fused_computation.48 | loop fusion | flops 11533312 | bytes 23076864 | tf_op jit(solution)/shard_map/reduce_sum | solution.py:284
  411.7 4.5 fusion.60
  416.3 5.3 fusion.29
  421.5 3.2 pad_maximum_fusion.2
  426.6 6.7 %convolution_convert_fusion = bf16[1536,1024]{1,0:T(8,128)(2,1)} fusion(bf16[1024,1536]{1,0:T(8,128)(2,1)S(1)} %copy-done.84, bf16[1024,1024]{1,0:T(8,128)(2,1)} %constant_dynamic-update-slice_fusion), kind=kOutput, calls=%fused_computation.70 | convolution fusion | flops 3222798336 | bytes 8388608 | tf_op jit(solution)/shard_map/dot_general | solution.py:52
  433.3 4.6 reshape.393
  437.9 6.5 %convolution_convert_fusion.2 = bf16[1024,1536]{1,0:T(8,128)(2,1)S(1)} fusion(bf16[1024,1536]{1,0:T(8,128)(2,1)} %copy-done.83, bf16[512,1024]{1,0:T(8,128)(2,1)} %collective-permute-done.2, bf16[512,1024]{1,0:T(8,128)(2,1)} %multiply_convert_fusion.4), kind=kOutput, calls=%fused_computation.72 | convolution fusion | flops 3226992640 | bytes 8388608 | tf_op jit(solution)/shard_map/dot_general | solution.py:52
  444.4 5.4 convolution_convert_fusion.1
  449.9 5.3 pad_maximum_fusion.1
  456.8 4.7 fusion.87
  467.8 19.8 %collective-permute-done.7 = bf16[512,1024]{1,0:T(8,128)(2,1)S(1)} collective-permute-done((bf16[512,1024]{1,0:T(8,128)(2,1)S(1)}, bf16[512,1024]{1,0:T(8,128)(2,1)S(1)}, u32[]{:S(2)}, u32[]{:S(2)}) %collective-permute-start.7) | collective-permute-done | bytes 1048608 | tf_op jit(solution)/shard_map/ppermute | solution.py:170
  487.6 2.7 multiply_reduce_fusion.3
  491.9 15.5 %collective-permute-done.8 = f32[18,128]{1,0:T(8,128)S(1)} collective-permute-done((f32[18,128]{1,0:T(8,128)S(1)}, f32[18,128]{1,0:T(8,128)S(1)}, u32[]{:S(2)}, u32[]{:S(2)}) %collective-permute-start.8) | collective-permute-done | bytes 9248 | tf_op jit(solution)/shard_map/ppermute | solution.py:139
  510.6 2.8 add_convert_fusion.2
  514.7 2.3 collective-permute-done.11
  518.8 2.3 multiply_add_fusion.1
  526.2 97.4 %reduce-scatter.5.cloned.1.call-done = bf16[64,4608]{1,0:T(8,128)(2,1)} async-done(((bf16[1024,4608]{1,0:T(8,128)(2,1)}), bf16[64,4608]{1,0:T(8,128)(2,1)}) %reduce-scatter.5.cloned.1.call-update) | async-done | bytes 589840 | tf_op jit(solution)/shard_map/reduce_scatter | solution.py:270
  623.6 2.1 fusion.131
  (314 shorter events, 88.8 us)
Async XLA Ops:
  7.2 8.1 %copy-start.76 = (s32[1024]{0:T(1024)S(1)}, s32[1024]{0:T(1024)}, u32[]{:S(2)}) copy-start(s32[1024]{0:T(1024)} %param.27) | copy-start | bytes 12292
  7.2 67.8 %all-gather.3.cloned.1.call-start = ((), (), s32[]{:S(2)}) async-start(), calls=%async_computation.2 | async-start | bytes 6684672 | tf_op jit(solution)/shard_map/all_gather | solution.py:206
  9.2 195.9 %all-gather.5.cloned.1.call-start = ((), (), s32[]{:S(2)}) async-start(), calls=%async_computation.3 | async-start | bytes 10027008 | tf_op jit(solution)/shard_map/all_gather | solution.py:207
  10.3 64.8 %copy-start.74 = (f32[1024]{0:T(1024)S(1)}, f32[1024]{0:T(1024)}, u32[]{:S(2)}) copy-start(f32[1024]{0:T(1024)} %param.28) | copy-start | bytes 12292
  12.2 510.6 %reduce-scatter.3.cloned.1.call-start = ((), (), s32[]{:S(2)}) async-start(), calls=%async_computation.4 | async-start | bytes 6684672 | tf_op jit(solution)/shard_map/reduce_scatter | solution.py:307
  12.2 26.2 %collective-permute-start = (bf16[512,1024]{1,0:T(8,128)(2,1)S(1)}, bf16[512,1024]{1,0:T(8,128)(2,1)S(1)}, u32[]{:S(2)}, u32[]{:S(2)}) collective-permute-start(bf16[512,1024]{1,0:T(8,128)(2,1)S(1)} %copy-done.40), channel_id=1, source_target_pairs={{0,1},{1,0},{2,3},{3,2},{4,5},{5,4},{6,7},{7,6},{8,9},{9,8},{10,11... | collective-permute-start | bytes 3145736 | tf_op jit(solution)/shard_map/ppermute | solution.py:150
  20.3 79.7 %copy-start.15 = (f32[1024,64]{1,0:T(8,128)}, f32[1024,64]{1,0:T(8,128)S(1)}, u32[]{:S(2)}) copy-start(f32[1024,64]{1,0:T(8,128)S(1)} %get-tuple-element.125) | copy-start | bytes 786436
  20.3 79.7 %copy-start.34 = (f32[1024,64]{1,0:T(8,128)}, f32[1024,64]{1,0:T(8,128)S(1)}, u32[]{:S(2)}) copy-start(f32[1024,64]{1,0:T(8,128)S(1)} %get-tuple-element.124) | copy-start | bytes 786436
  38.5 46.6 %copy-start.44 = (bf16[512,1024]{1,0:T(8,128)(2,1)}, bf16[512,1024]{1,0:T(8,128)(2,1)S(1)}, u32[]{:S(2)}) copy-start(bf16[512,1024]{1,0:T(8,128)(2,1)S(1)} %collective-permute-done) | copy-start | bytes 3145732
  39.0 46.1 %copy-start.67 = (f32[1024]{0:T(1024)}, f32[1024]{0:T(1024)S(1)}, u32[]{:S(2)}) copy-start(f32[1024]{0:T(1024)S(1)} %add_rsqrt_fusion.2) | copy-start | bytes 12292
  89.4 15.4 %copy-start.1 = (f32[512,2048]{1,0:T(8,128)}, f32[512,2048]{1,0:T(8,128)S(1)}, u32[]{:S(2)}) copy-start(f32[512,2048]{1,0:T(8,128)S(1)} %get-tuple-element.90) | copy-start | bytes 12582916
  89.4 15.4 %copy-start.3 = (f32[512,2048]{1,0:T(8,128)}, f32[512,2048]{1,0:T(8,128)S(1)}, u32[]{:S(2)}) copy-start(f32[512,2048]{1,0:T(8,128)S(1)} %get-tuple-element.91) | copy-start | bytes 12582916
  105.1 12.8 %copy-start.8 = (f32[1024,512]{1,0:T(8,128)}, f32[1024,512]{1,0:T(8,128)S(1)}, u32[]{:S(2)}) copy-start(f32[1024,512]{1,0:T(8,128)S(1)} %fusion.50) | copy-start | bytes 6291460
  107.3 7.5 %slice-start.10 = ((bf16[1024,2048]{1,0:T(8,128)(2,1)}), bf16[1024,512]{1,0:T(8,128)(2,1)S(1)}, s32[]{:S(2)}) async-start(bf16[1024,2048]{1,0:T(8,128)(2,1)} %fusion.5), calls=%async_computation.16 | async-start | bytes 2097152 | tf_op jit(solution)/shard_map/slice | solution.py:232
  117.9 161.4 %copy-start.60 = (f32[1024,4]{0,1:T(4,128)}, f32[1024,4]{0,1:T(4,128)S(1)}, u32[]{:S(2)}) copy-start(f32[1024,4]{0,1:T(4,128)S(1)} %add_rsqrt_fusion.1) | copy-start | bytes 49156
  133.2 8.3 %copy-start.38 = (bf16[1024,4,128]{2,1,0:T(4,128)(2,1)S(1)}, bf16[1024,4,128]{2,1,0:T(4,128)(2,1)}, u32[]{:S(2)}) copy-start(bf16[1024,4,128]{2,1,0:T(4,128)(2,1)} %reshape.387) | copy-start | bytes 3145732
  133.2 16.2 %slice-start = ((s8[8388608]{0:T(1024)(128)(4,1)}), s8[4194304]{0:T(1024)(128)(4,1)S(1)}, s32[]{:S(2)}) async-start(s8[8388608]{0:T(1024)(128)(4,1)} %bitcast.212), calls=%async_computation.6 | async-start | bytes 8388608
  141.5 7.8 %slice-start.1 = ((s8[8388608]{0:T(1024)(128)(4,1)}), s8[4194304]{0:T(1024)(128)(4,1)S(1)}, s32[]{:S(2)}) async-start(s8[8388608]{0:T(1024)(128)(4,1)} %bitcast.212), calls=%async_computation.7 | async-start | bytes 8388608
  141.5 7.8 %copy-start.50 = (bf16[512,4,128]{2,1,0:T(4,128)(2,1)S(1)}, bf16[512,4,128]{2,1,0:T(4,128)(2,1)}, u32[]{:S(2)}) copy-start(bf16[512,4,128]{2,1,0:T(4,128)(2,1)} %slice.274) | copy-start | bytes 1572868
  151.8 29.8 %copy-start.79 = (bf16[4,128,2,512]{3,1,2,0:T(8,128)(2,1)}, bf16[4,128,2,512]{3,1,2,0:T(8,128)(2,1)S(1)}, u32[]{:S(2)}) copy-start(bf16[4,128,2,512]{3,1,2,0:T(8,128)(2,1)S(1)} %get-tuple-element.110) | copy-start | bytes 3145732
  151.8 29.8 %copy-start.41 = (bf16[512,1024]{1,0:T(8,128)(2,1)S(1)}, bf16[512,1024]{1,0:T(8,128)(2,1)}, u32[]{:S(2)}) copy-start(bf16[512,1024]{1,0:T(8,128)(2,1)} %param.26) | copy-start | bytes 3145732
  155.5 26.1 %collective-permute-start.1 = (bf16[512,1024]{1,0:T(8,128)(2,1)S(1)}, bf16[512,1024]{1,0:T(8,128)(2,1)S(1)}, u32[]{:S(2)}, u32[]{:S(2)}) collective-permute-start(bf16[512,1024]{1,0:T(8,128)(2,1)S(1)} %fusion.84), channel_id=1, source_target_pairs={{0,1},{1,0},{2,3},{3,2},{4,5},{5,4},{6,7},{7,6},{8,9},{9,8},{10,11... | collective-permute-start | bytes 3145736 | tf_op jit(solution)/shard_map/ppermute | solution.py:170
  157.1 46.9 %collective-permute-start.4 = (bf16[512,1024]{1,0:T(8,128)(2,1)S(1)}, bf16[512,1024]{1,0:T(8,128)(2,1)S(1)}, u32[]{:S(2)}, u32[]{:S(2)}) collective-permute-start(bf16[512,1024]{1,0:T(8,128)(2,1)S(1)} %copy-done.23), channel_id=1, source_target_pairs={{0,1},{1,0},{2,3},{3,2},{4,5},{5,4},{6,7},{7,6},{8,9},{9,8},{10,11... | collective-permute-start | bytes 3145736 | tf_op jit(solution)/shard_map/ppermute | solution.py:150
  184.7 91.4 %copy-start.10 = (f32[512,1024]{1,0:T(8,128)}, f32[512,1024]{1,0:T(8,128)S(1)}, u32[]{:S(2)}) copy-start(f32[512,1024]{1,0:T(8,128)S(1)} %get-tuple-element.131) | copy-start | bytes 6291460
  184.7 91.4 %copy-start.65 = (f32[512]{0:T(512)}, f32[512]{0:T(512)S(1)}, u32[]{:S(2)}) copy-start(f32[512]{0:T(512)S(1)} %add_rsqrt_fusion.3) | copy-start | bytes 6148
  186.3 39.6 %collective-permute-start.2 = (bf16[512,1024]{1,0:T(8,128)(2,1)}, bf16[512,1024]{1,0:T(8,128)(2,1)}, u32[]{:S(2)}, u32[]{:S(2)}) collective-permute-start(bf16[512,1024]{1,0:T(8,128)(2,1)} %multiply_convert_fusion.4), channel_id=1, source_target_pairs={{0,1},{1,0},{2,3},{3,2},{4,5},{5,4},{6,7},{7,6},{8,9},{9,8},{10,11... | collective-permute-start | bytes 3145736 | tf_op jit(solution)/shard_map/ppermute | solution.py:150
  214.7 19.8 %slice-start.11 = ((s8[9437184]{0:T(1024)(128)(4,1)}), s8[4194304]{0:T(1024)(128)(4,1)S(1)}, s32[]{:S(2)}) async-start(s8[9437184]{0:T(1024)(128)(4,1)} %bitcast.241), calls=%async_computation.17 | async-start | bytes 8388608
  214.7 19.8 %slice-start.12 = ((s8[9437184]{0:T(1024)(128)(4,1)}), s8[4194304]{0:T(1024)(128)(4,1)S(1)}, s32[]{:S(2)}) async-start(s8[9437184]{0:T(1024)(128)(4,1)} %bitcast.241), calls=%async_computation.18 | async-start | bytes 8388608
  223.5 11.0 %slice-start.13 = ((s8[9437184]{0:T(1024)(128)(4,1)}), s8[1048576]{0:T(1024)(128)(4,1)S(1)}, s32[]{:S(2)}) async-start(s8[9437184]{0:T(1024)(128)(4,1)} %bitcast.241), calls=%async_computation.19 | async-start | bytes 2097152
  245.1 28.2 %copy-start.83 = (bf16[1024,1536]{1,0:T(8,128)(2,1)}, bf16[1024,1536]{1,0:T(8,128)(2,1)S(1)}, u32[]{:S(2)}) copy-start(bf16[1024,1536]{1,0:T(8,128)(2,1)S(1)} %get-tuple-element.85) | copy-start | bytes 9437188
  248.8 24.5 %collective-permute-start.5 = (bf16[512,1024]{1,0:T(8,128)(2,1)S(1)}, bf16[512,1024]{1,0:T(8,128)(2,1)S(1)}, u32[]{:S(2)}, u32[]{:S(2)}) collective-permute-start(bf16[512,1024]{1,0:T(8,128)(2,1)S(1)} %add_convert_fusion.1), channel_id=1, source_target_pairs={{0,1},{1,0},{2,3},{3,2},{4,5},{5,4},{6,7},{7,6},{8,9},{9,8},{10,11... | collective-permute-start | bytes 3145736 | tf_op jit(solution)/shard_map/ppermute | solution.py:170
  252.2 24.0 %copy-start.24 = (bf16[512,1024]{1,0:T(8,128)(2,1)S(1)}, bf16[512,1024]{1,0:T(8,128)(2,1)}, u32[]{:S(2)}) copy-start(bf16[512,1024]{1,0:T(8,128)(2,1)} %param.39) | copy-start | bytes 3145732
  277.8 23.8 %collective-permute-start.6 = (bf16[512,1024]{1,0:T(8,128)(2,1)}, bf16[512,1024]{1,0:T(8,128)(2,1)S(1)}, u32[]{:S(2)}, u32[]{:S(2)}) collective-permute-start(bf16[512,1024]{1,0:T(8,128)(2,1)} %fusion.128), channel_id=1, source_target_pairs={{0,1},{1,0},{2,3},{3,2},{4,5},{5,4},{6,7},{7,6},{8,9},{9,8},{10,11... | collective-permute-start | bytes 3145736 | tf_op jit(solution)/shard_map/ppermute | solution.py:150
  280.3 27.1 %slice-start.2 = ((s8[8388608]{0:T(1024)(128)(4,1)}), s8[4194304]{0:T(1024)(128)(4,1)S(1)}, s32[]{:S(2)}) async-start(s8[8388608]{0:T(1024)(128)(4,1)} %bitcast.214), calls=%async_computation.8 | async-start | bytes 8388608
  281.0 26.5 %slice-start.3 = ((s8[8388608]{0:T(1024)(128)(4,1)}), s8[4194304]{0:T(1024)(128)(4,1)S(1)}, s32[]{:S(2)}) async-start(s8[8388608]{0:T(1024)(128)(4,1)} %bitcast.214), calls=%async_computation.9 | async-start | bytes 8388608
  309.4 9.9 %slice-start.4 = ((s8[16777216]{0:T(1024)(128)(4,1)}), s8[4194304]{0:T(1024)(128)(4,1)S(1)}, s32[]{:S(2)}) async-start(s8[16777216]{0:T(1024)(128)(4,1)} %bitcast.216), calls=%async_computation.10 | async-start | bytes 8388608
  309.4 9.8 %slice-start.5 = ((s8[16777216]{0:T(1024)(128)(4,1)}), s8[4194304]{0:T(1024)(128)(4,1)S(1)}, s32[]{:S(2)}) async-start(s8[16777216]{0:T(1024)(128)(4,1)} %bitcast.216), calls=%async_computation.11 | async-start | bytes 8388608
  312.1 7.1 %slice-start.6 = ((s8[16777216]{0:T(1024)(128)(4,1)}), s8[4194304]{0:T(1024)(128)(4,1)S(1)}, s32[]{:S(2)}) async-start(s8[16777216]{0:T(1024)(128)(4,1)} %bitcast.216), calls=%async_computation.12 | async-start | bytes 8388608
  330.5 8.4 %copy-start.14 = (bf16[1024,4,64]{2,0,1:T(8,128)(2,1)S(1)}, bf16[1024,4,64]{2,0,1:T(8,128)(2,1)}, u32[]{:S(2)}) copy-start(bf16[1024,4,64]{2,0,1:T(8,128)(2,1)} %copy-done.12) | copy-start | bytes 1572868
  351.2 22.7 %slice-start.8 = ((s8[8388608]{0:T(1024)(128)(4,1)}), s8[4194304]{0:T(1024)(128)(4,1)S(1)}, s32[]{:S(2)}) async-start(s8[8388608]{0:T(1024)(128)(4,1)} %bitcast.218), calls=%async_computation.14 | async-start | bytes 8388608
  355.9 17.9 %slice-start.9 = ((s8[8388608]{0:T(1024)(128)(4,1)}), s8[4194304]{0:T(1024)(128)(4,1)S(1)}, s32[]{:S(2)}) async-start(s8[8388608]{0:T(1024)(128)(4,1)} %bitcast.218), calls=%async_computation.15 | async-start | bytes 8388608
  355.9 17.9 %copy-start.37 = (bf16[512,8,128]{2,0,1:T(8,128)(2,1)S(1)}, bf16[512,8,128]{2,0,1:T(8,128)(2,1)}, u32[]{:S(2)}) copy-start(bf16[512,8,128]{2,0,1:T(8,128)(2,1)} %copy.156) | copy-start | bytes 3145732
  356.0 17.9 %copy-start.39 = (f32[512,4,128]{2,0,1:T(8,128)S(1)}, f32[512,4,128]{2,0,1:T(8,128)}, u32[]{:S(2)}) copy-start(f32[512,4,128]{2,0,1:T(8,128)} %fusion.104) | copy-start | bytes 3145732
  398.5 7.0 %copy-start.53 = (f32[1024,4]{1,0:T(8,128)S(1)}, f32[1024,4]{1,0:T(8,128)}, u32[]{:S(2)}) copy-start(f32[1024,4]{1,0:T(8,128)} %copy.177) | copy-start | bytes 49156
  398.5 8.3 %copy-start.52 = (f32[1024,4]{1,0:T(8,128)S(1)}, f32[1024,4]{1,0:T(8,128)}, u32[]{:S(2)}) copy-start(f32[1024,4]{1,0:T(8,128)} %copy.228) | copy-start | bytes 49156
  424.7 198.9 %reduce-scatter.5.cloned.1.call-start = ((), (), s32[]{:S(2)}) async-start(), calls=%async_computation.5 | async-start | bytes 10027008 | tf_op jit(solution)/shard_map/reduce_scatter | solution.py:270
  461.5 26.1 %collective-permute-start.7 = (bf16[512,1024]{1,0:T(8,128)(2,1)S(1)}, bf16[512,1024]{1,0:T(8,128)(2,1)S(1)}, u32[]{:S(2)}, u32[]{:S(2)}) collective-permute-start(bf16[512,1024]{1,0:T(8,128)(2,1)S(1)} %fusion.87), channel_id=1, source_target_pairs={{0,1},{1,0},{2,3},{3,2},{4,5},{5,4},{6,7},{7,6},{8,9},{9,8},{10,11... | collective-permute-start | bytes 3145736 | tf_op jit(solution)/shard_map/ppermute | solution.py:170
  463.0 24.5 %slice-start.15 = ((s8[6291456]{0:T(1024)(128)(4,1)}), s8[4194304]{0:T(1024)(128)(4,1)S(1)}, s32[]{:S(2)}) async-start(s8[6291456]{0:T(1024)(128)(4,1)} %bitcast.253), calls=%async_computation.21 | async-start | bytes 8388608
  464.3 23.2 %copy-start.55 = (bf16[512,2048]{1,0:T(8,128)(2,1)S(1)}, bf16[512,2048]{1,0:T(8,128)(2,1)}, u32[]{:S(2)}) copy-start(bf16[512,2048]{1,0:T(8,128)(2,1)} %copy-done.54) | copy-start | bytes 6291460
  464.3 23.2 %slice-start.16 = ((s8[6291456]{0:T(1024)(128)(4,1)}), s8[2097152]{0:T(1024)(128)(4,1)S(1)}, s32[]{:S(2)}) async-start(s8[6291456]{0:T(1024)(128)(4,1)} %bitcast.253), calls=%async_computation.22 | async-start | bytes 4194304
  466.1 44.4 %collective-permute-start.3 = (bf16[512,1024]{1,0:T(8,128)(2,1)S(1)}, bf16[512,1024]{1,0:T(8,128)(2,1)S(1)}, u32[]{:S(2)}, u32[]{:S(2)}) collective-permute-start(bf16[512,1024]{1,0:T(8,128)(2,1)S(1)} %fusion.81), channel_id=1, source_target_pairs={{0,1},{1,0},{2,3},{3,2},{4,5},{5,4},{6,7},{7,6},{8,9},{9,8},{10,11... | collective-permute-start | bytes 3145736 | tf_op jit(solution)/shard_map/ppermute | solution.py:170
  467.7 22.6 %copy-start.64 = (f32[1024]{0:T(1024)S(1)}, f32[1024]{0:T(1024)}, u32[]{:S(2)}) copy-start(f32[1024]{0:T(1024)} %get-tuple-element.79) | copy-start | bytes 12292
  467.7 42.8 %copy-start.11 = (f32[512,1024]{1,0:T(8,128)S(1)}, f32[512,1024]{1,0:T(8,128)}, u32[]{:S(2)}) copy-start(f32[512,1024]{1,0:T(8,128)} %copy-done.10) | copy-start | bytes 6291460
  490.3 17.1 %collective-permute-start.8 = (f32[18,128]{1,0:T(8,128)S(1)}, f32[18,128]{1,0:T(8,128)S(1)}, u32[]{:S(2)}, u32[]{:S(2)}) collective-permute-start(f32[18,128]{1,0:T(8,128)S(1)} %maximum_bitcast_fusion.3), channel_id=1, source_target_pairs={{0,1},{1,0},{2,3},{3,2},{4,5},{5,4},{6,7},{7,6},{8,9},{9,8},{10,11... | collective-permute-start | bytes 27656 | tf_op jit(solution)/shard_map/ppermute | solution.py:139
  507.5 1.2 collective-permute-start.9
  508.6 10.1 %copy-start.25 = (bf16[512,1024]{1,0:T(8,128)(2,1)S(1)}, bf16[512,1024]{1,0:T(8,128)(2,1)}, u32[]{:S(2)}) copy-start(bf16[512,1024]{1,0:T(8,128)(2,1)} %param.39) | copy-start | bytes 3145732
  508.7 10.1 %copy-start.30 = (f32[512,1024]{1,0:T(8,128)S(1)}, f32[512,1024]{1,0:T(8,128)}, u32[]{:S(2)}) copy-start(f32[512,1024]{1,0:T(8,128)} %copy-done.29) | copy-start | bytes 6291460
  508.7 10.1 %copy-start.63 = (f32[1024]{0:T(1024)S(1)}, f32[1024]{0:T(1024)}, u32[]{:S(2)}) copy-start(f32[1024]{0:T(1024)} %param.29) | copy-start | bytes 12292
  508.7 10.1 %copy-start.66 = (f32[512]{0:T(512)S(1)}, f32[512]{0:T(512)}, u32[]{:S(2)}) copy-start(f32[512]{0:T(512)} %copy-done.65) | copy-start | bytes 6148
  508.7 10.1 %slice-start.14 = ((f32[1024]{0:T(1024)}), f32[512]{0:T(512)S(1)}, s32[]{:S(2)}) async-start(f32[1024]{0:T(1024)} %copy-done.67), calls=%async_computation.20 | async-start | bytes 4096 | tf_op jit(solution)/shard_map/slice | solution.py:221
  508.7 10.1 %copy-start.70 = (f32[512]{0:T(512)S(1)}, f32[512]{0:T(512)}, u32[]{:S(2)}) copy-start(f32[512]{0:T(512)} %copy-done.69) | copy-start | bytes 6148
  508.7 4.6 collective-permute-start.10
  513.3 3.7 collective-permute-start.11
  517.0 4.6 collective-permute-start.12
  (59 other events, 186.7 us)
Sparse Core Ops, SparseCore 0:
  10.9 64.1 all-gather.2
  77.3 79.5 all-gather.4
  424.8 84.4 reduce-scatter.2
  513.3 110.3 reduce-scatter.4
where the time goes:
time: 643 us; the launch traced here: 634 us
  waiting for transfers between devices  274 us (43%)
  matrix products  152 us (24%)
  other arithmetic  101 us (16%)
  local copies, waits for them, and re-layouts  70.6 us (11%)
  starting transfers between devices  19.5 us (3%)
  between operations  15.5 us (2%)
    reduce_scatter x1, waiting for transfers between devices, local(): lax.psum_scatter(grad_mlp_w, 'dp', scatter_dimension=0, tiled=True)  97.4 us
    ppermute x4, waiting for transfers between devices, scatter_rows(): got = lax.ppermute(sent, 'tensor', swap)  64.9 us
    ppermute x4, waiting for transfers between devices, gather_rows(): return jnp.concatenate((own, lax.ppermute(own, 'tensor', swap)), 0)  56.4 us
    dot_general x7, matrix products, matmul(): return jnp.dot(left, right, preferred_element_type=F32)  40.6 us
    all_gather x1, waiting for transfers between devices, local(): full_attn = lax.all_gather(shard_attn, 'dp', axis=0, tiled=True)  36.1 us
    dot_general x8, matrix products, contract_cols(): lax.dot_general(left, right, (((1,), (1,)), ((), ())), preferred_element_...  29.2 us
    dot_general x5, matrix products, contract_rows(): lax.dot_general(left, right, (((0,), (0,)), ((), ())), preferred_element_...  28.4 us
    unnamed x213, local copies, waits for them, and re-layouts  23.4 us
  transfers between devices with their start and end apart: 17, of which 13 were waited for; matrix products, arithmetic and copies ran while one was open for 26% of the time, Pallas kernels for 0%

commit v1 on v0

--- a/solution.py
+++ b/solution.py
@@ -203,7 +203,14 @@
             (query_proj, key_proj, value_proj, out_proj.reshape(shard_rows, -1)), 1
         )
         shard_mlp = jnp.concatenate((gate_proj, up_proj, down_proj.reshape(shard_rows, -1)), 1)
-        full_attn = lax.all_gather(shard_attn, "dp", axis=0, tiled=True)
+        ring = [shard_attn]
+        for hop in range(15):
+            ring.append(lax.ppermute(ring[-1], "dp", [(dev, (dev + 1) % 16) for dev in range(16)]))
+        full_attn = jnp.roll(
+            jnp.concatenate(ring[::-1], axis=0),
+            (lax.axis_index("dp") + 1) * ring[0].shape[0],
+            axis=0,
+        )
         full_mlp = lax.all_gather(shard_mlp, "dp", axis=0, tiled=True)
         proj_qkv = full_attn[:, :width_qkv]
         full_out = full_attn[:, width_qkv:].reshape(-1, width)

time: 643 us -> 730 us (1.14)
  waiting for transfers between devices: 274 us -> 350 us
  local copies, waits for them, and re-layouts: 70.6 us -> 86.5 us
    ppermute x0 -> x15, waiting for transfers between devices: none -> 151 us  [local(): lax.ppermute(ring[-1], 'dp', [(dev, (dev + 1) % 16) for dev in range(16)])]
    all_gather x1 -> x0, waiting for transfers between devices: 36.1 us -> none  [local(): full_attn = lax.all_gather(shard_attn, 'dp', axis=0, tiled=True)]
    ppermute x4, waiting for transfers between devices: 56.4 us -> 22.1 us  [gather_rows(): return jnp.concatenate((own, lax.ppermute(own, 'tensor', swap)), 0)]
    ppermute x4, waiting for transfers between devices: 64.9 us -> 48 us  [scatter_rows(): got = lax.ppermute(sent, 'tensor', swap)]
    unnamed x213 -> x288, local copies, waits for them, and re-layouts: 23.4 us -> 37.7 us
    reduce_scatter x1, waiting for transfers between devices: 97.4 us -> 111 us  [local(): lax.psum_scatter(grad_mlp_w, 'dp', scatter_dimension=0, tiled=True)]
    ppermute x5, waiting for transfers between devices: 19.6 us -> 11.4 us  [all_sum(): lax.ppermute(value, axis, [(i, i ^ step) for i in range(size)])]
  transfers between devices with their start and end apart: 17 -> 31, of which waited for: 13 -> 26; matrix products, arithmetic and copies ran while one was open for 26% -> 24% of each run, Pallas kernels for 0% -> 0%
where the time goes in v1:
time: 730 us; the launch traced here: 725 us
  waiting for transfers between devices  350 us (48%)
  matrix products  151 us (21%)
  other arithmetic  102 us (14%)
  local copies, waits for them, and re-layouts  86.5 us (12%)
  starting transfers between devices  18.6 us (3%)
  between operations  15.8 us (2%)
    ppermute x15, waiting for transfers between devices, local(): lax.ppermute(ring[-1], 'dp', [(dev, (dev + 1) % 16) for dev in range(16)])  151 us
    reduce_scatter x1, waiting for transfers between devices, local(): lax.psum_scatter(grad_mlp_w, 'dp', scatter_dimension=0, tiled=True)  111 us
    ppermute x4, waiting for transfers between devices, scatter_rows(): got = lax.ppermute(sent, 'tensor', swap)  48 us
    dot_general x7, matrix products, matmul(): return jnp.dot(left, right, preferred_element_type=F32)  38 us
    unnamed x288, local copies, waits for them, and re-layouts  37.7 us
    dot_general x8, matrix products, contract_cols(): lax.dot_general(left, right, (((1,), (1,)), ((), ())), preferred_element_...  31.3 us
    dot_general x5, matrix products, contract_rows(): lax.dot_general(left, right, (((0,), (0,)), ((), ())), preferred_element_...  28.3 us
    ppermute x4, waiting for transfers between devices, gather_rows(): return jnp.concatenate((own, lax.ppermute(own, 'tensor', swap)), 0)  22.1 us
  transfers between devices with their start and end apart: 31, of which 26 were waited for; matrix products, arithmetic and copies ran while one was open for 24% of the time, Pallas kernels for 0%

profile of v1, /device:TPU:0, one launch (start us, length us, event | category | flops | bytes accessed | tf_op | source)
XLA Modules:
  0.0 724.7 jit_solution(12587783999064189599)
XLA Ops:
  8.9 10.4 %collective-permute-done.1 = bf16[64,3072]{1,0:T(8,128)(2,1)S(1)} collective-permute-done((bf16[64,3072]{1,0:T(8,128)(2,1)S(1)}, bf16[64,3072]{1,0:T(8,128)(2,1)S(1)}, u32[]{:S(2)}, u32[]{:S(2)}) %collective-permute-start.1) | collective-permute-done | bytes 393248 | tf_op jit(solution)/shard_map/ppermute | solution.py:208
  19.3 9.9 %collective-permute-done.2 = bf16[64,3072]{1,0:T(8,128)(2,1)S(1)} collective-permute-done((bf16[64,3072]{1,0:T(8,128)(2,1)S(1)}, bf16[64,3072]{1,0:T(8,128)(2,1)S(1)}, u32[]{:S(2)}, u32[]{:S(2)}) %collective-permute-start.2) | collective-permute-done | bytes 393248 | tf_op jit(solution)/shard_map/ppermute | solution.py:208
  29.2 9.9 %collective-permute-done.3 = bf16[64,3072]{1,0:T(8,128)(2,1)S(1)} collective-permute-done((bf16[64,3072]{1,0:T(8,128)(2,1)S(1)}, bf16[64,3072]{1,0:T(8,128)(2,1)S(1)}, u32[]{:S(2)}, u32[]{:S(2)}) %collective-permute-start.3) | collective-permute-done | bytes 393248 | tf_op jit(solution)/shard_map/ppermute | solution.py:208
  39.1 9.9 %collective-permute-done.4 = bf16[64,3072]{1,0:T(8,128)(2,1)S(1)} collective-permute-done((bf16[64,3072]{1,0:T(8,128)(2,1)S(1)}, bf16[64,3072]{1,0:T(8,128)(2,1)S(1)}, u32[]{:S(2)}, u32[]{:S(2)}) %collective-permute-start.4) | collective-permute-done | bytes 393248 | tf_op jit(solution)/shard_map/ppermute | solution.py:208
  49.0 9.9 %collective-permute-done.5 = bf16[64,3072]{1,0:T(8,128)(2,1)S(1)} collective-permute-done((bf16[64,3072]{1,0:T(8,128)(2,1)S(1)}, bf16[64,3072]{1,0:T(8,128)(2,1)S(1)}, u32[]{:S(2)}, u32[]{:S(2)}) %collective-permute-start.5) | collective-permute-done | bytes 393248 | tf_op jit(solution)/shard_map/ppermute | solution.py:208
  58.9 9.9 %collective-permute-done.6 = bf16[64,3072]{1,0:T(8,128)(2,1)S(1)} collective-permute-done((bf16[64,3072]{1,0:T(8,128)(2,1)S(1)}, bf16[64,3072]{1,0:T(8,128)(2,1)S(1)}, u32[]{:S(2)}, u32[]{:S(2)}) %collective-permute-start.6) | collective-permute-done | bytes 393248 | tf_op jit(solution)/shard_map/ppermute | solution.py:208
  68.8 9.9 %collective-permute-done.7 = bf16[64,3072]{1,0:T(8,128)(2,1)S(1)} collective-permute-done((bf16[64,3072]{1,0:T(8,128)(2,1)S(1)}, bf16[64,3072]{1,0:T(8,128)(2,1)S(1)}, u32[]{:S(2)}, u32[]{:S(2)}) %collective-permute-start.7) | collective-permute-done | bytes 393248 | tf_op jit(solution)/shard_map/ppermute | solution.py:208
  78.7 9.9 %collective-permute-done.8 = bf16[64,3072]{1,0:T(8,128)(2,1)S(1)} collective-permute-done((bf16[64,3072]{1,0:T(8,128)(2,1)S(1)}, bf16[64,3072]{1,0:T(8,128)(2,1)S(1)}, u32[]{:S(2)}, u32[]{:S(2)}) %collective-permute-start.8) | collective-permute-done | bytes 393248 | tf_op jit(solution)/shard_map/ppermute | solution.py:208
  88.6 9.9 %collective-permute-done.9 = bf16[64,3072]{1,0:T(8,128)(2,1)S(1)} collective-permute-done((bf16[64,3072]{1,0:T(8,128)(2,1)S(1)}, bf16[64,3072]{1,0:T(8,128)(2,1)S(1)}, u32[]{:S(2)}, u32[]{:S(2)}) %collective-permute-start.9) | collective-permute-done | bytes 393248 | tf_op jit(solution)/shard_map/ppermute | solution.py:208
  98.6 9.9 %collective-permute-done.10 = bf16[64,3072]{1,0:T(8,128)(2,1)S(1)} collective-permute-done((bf16[64,3072]{1,0:T(8,128)(2,1)S(1)}, bf16[64,3072]{1,0:T(8,128)(2,1)S(1)}, u32[]{:S(2)}, u32[]{:S(2)}) %collective-permute-start.10) | collective-permute-done | bytes 393248 | tf_op jit(solution)/shard_map/ppermute | solution.py:208
  108.5 10.0 %collective-permute-done.11 = bf16[64,3072]{1,0:T(8,128)(2,1)} collective-permute-done((bf16[64,3072]{1,0:T(8,128)(2,1)S(1)}, bf16[64,3072]{1,0:T(8,128)(2,1)}, u32[]{:S(2)}, u32[]{:S(2)}) %collective-permute-start.11) | collective-permute-done | bytes 393248 | tf_op jit(solution)/shard_map/ppermute | solution.py:208
  122.4 6.4 collective-permute-done.12
  130.8 8.1 %collective-permute-done.13 = bf16[64,3072]{1,0:T(8,128)(2,1)} collective-permute-done((bf16[64,3072]{1,0:T(8,128)(2,1)}, bf16[64,3072]{1,0:T(8,128)(2,1)}, u32[]{:S(2)}, u32[]{:S(2)}) %collective-permute-start.13) | collective-permute-done | bytes 393248 | tf_op jit(solution)/shard_map/ppermute | solution.py:208
  140.8 3.0 fusion.117
  143.8 10.6 %collective-permute-done.14 = bf16[64,3072]{1,0:T(8,128)(2,1)} collective-permute-done((bf16[64,3072]{1,0:T(8,128)(2,1)}, bf16[64,3072]{1,0:T(8,128)(2,1)}, u32[]{:S(2)}, u32[]{:S(2)}) %collective-permute-start.14) | collective-permute-done | bytes 393248 | tf_op jit(solution)/shard_map/ppermute | solution.py:208
  155.7 16.7 %collective-permute-done.15 = bf16[64,3072]{1,0:T(8,128)(2,1)} collective-permute-done((bf16[64,3072]{1,0:T(8,128)(2,1)}, bf16[64,3072]{1,0:T(8,128)(2,1)}, u32[]{:S(2)}, u32[]{:S(2)}) %collective-permute-start.15) | collective-permute-done | bytes 393248 | tf_op jit(solution)/shard_map/ppermute | solution.py:208
  184.5 4.6 copy-done.92
  189.1 7.2 fusion.36
  196.3 4.4 slice_select_fusion.1
  206.8 3.6 multiply_reduce_fusion.8
  211.6 2.8 fusion.132
  238.0 7.5 %fusion.138 = (f32[4,2,512]{2,1,0:T(2,128)S(1)}, f32[4,2,512,1024]{2,3,1,0:T(8,128)}) fusion(bf16[512,4,2,128]{3,0,2,1:T(8,128)(2,1)S(1)} %bitcast.234, bf16[1024,4,64]{2,0,1:T(8,128)(2,1)S(1)} %get-tuple-element.107, bf16[1024,4,64]{2,0,1:T(8,128)(2,1)S(1)} %get-tuple-element.106, pred[512,1024]{0,1:T(8,128)(4,1)S(1)} %copy-done.79), kind=kOutput, calls=%fused_computation.267 | convolution fusion | flops 1088417792 | bytes 19415040 | tf_op jit(solution)/shard_map/qgrd,kgd->grqk/dot_general | solution.py:71
  245.5 8.2 %fusion.3 = f32[4,2,512]{2,1,0:T(2,128)S(1)} fusion(f32[4,2,512,1024]{2,3,1,0:T(8,128)} %get-tuple-element.129, f32[4,2,512]{2,1,0:T(2,128)S(1)} %get-tuple-element.128), kind=kLoop, calls=%fused_computation.9 | loop fusion | flops 8384512 | bytes 16809984 | tf_op jit(solution)/shard_map/reduce_sum | solution.py:80
  253.7 7.8 %fusion.80 = bf16[4,128,2,512]{3,1,2,0:T(8,128)(2,1)S(1)} fusion(f32[4,2,512,1024]{2,3,1,0:T(8,128)} %get-tuple-element.129, f32[4,2,512]{2,1,0:T(2,128)S(1)} %fusion.3, f32[4,2,512]{2,1,0:T(2,128)S(1)} %get-tuple-element.128, bf16[1024,4,128,1]{2,1,0,3:T(4,128)(2,1)S(1)} %bitcast.237), kind=kOutput, calls=%fused_computation.156 | convolution fusion | flops 1086849024 | bytes 18907136 | tf_op jit(solution)/shard_map/grqk,kgd->qgrd/dot_general | solution.py:83
  263.6 3.6 fusion.84
  269.3 24.0 %collective-permute-done.16 = bf16[512,1024]{1,0:T(8,128)(2,1)S(1)} collective-permute-done((bf16[512,1024]{1,0:T(8,128)(2,1)S(1)}, bf16[512,1024]{1,0:T(8,128)(2,1)S(1)}, u32[]{:S(2)}, u32[]{:S(2)}) %collective-permute-start.16) | collective-permute-done | bytes 1048608 | tf_op jit(solution)/shard_map/ppermute | solution.py:170
  293.3 3.2 multiply_reduce_fusion.7
  301.0 10.3 %collective-permute-done.19 = bf16[512,1024]{1,0:T(8,128)(2,1)S(1)} collective-permute-done((bf16[512,1024]{1,0:T(8,128)(2,1)S(1)}, bf16[512,1024]{1,0:T(8,128)(2,1)S(1)}, u32[]{:S(2)}, u32[]{:S(2)}) %collective-permute-start.19) | collective-permute-done | bytes 1048608 | tf_op jit(solution)/shard_map/ppermute | solution.py:150
  312.3 3.8 slice.343
  316.0 6.1 reshape.389
  322.1 8.7 %fusion.139 = f32[1024,1536]{1,0:T(8,128)} fusion(bf16[1024,1024]{1,0:T(8,128)(2,1)} %constant_dynamic-update-slice_fusion.32, bf16[1536,1024]{1,0:T(8,128)(2,1)} %reshape.389), kind=kOutput, calls=%fused_computation.268 | convolution fusion | flops 3221225472 | bytes 11534336 | tf_op jit(solution)/shard_map/dot_general | solution.py:56
  330.9 8.6 %fusion.42 = f32[1024,1536]{1,0:T(8,128)} fusion(bf16[1024,4608]{1,0:T(8,128)(2,1)} %all-gather.2.cloned.1.call-done, bf16[512,1024]{1,0:T(8,128)(2,1)} %collective-permute-done.17, bf16[512,1024]{1,0:T(8,128)(2,1)} %multiply_convert_fusion.4), kind=kOutput, calls=%fused_computation.83 | convolution fusion | flops 3225419776 | bytes 11534336 | tf_op jit(solution)/shard_map/dot_general | solution.py:48
  339.5 10.9 %multiply_convert_fusion.1 = (bf16[1024,1536]{1,0:T(8,128)(2,1)S(1)}, bf16[1024,1536]{1,0:T(8,128)(2,1)}, bf16[1024,1536]{1,0:T(8,128)(2,1)S(1)}) fusion(f32[1024,1536]{1,0:T(8,128)} %fusion.139, f32[1024,1536]{1,0:T(8,128)} %fusion.42, bf16[1024,4608]{1,0:T(8,128)(2,1)S(1)} %bitcast.242, bf16[512,1024]{1,0:T(8,128)(2,1)} %collective-permute-done.17, ...), kind=kOutput, calls=%fused_computation.34 | convolution fusion | flops 3250585600 | bytes 27262976 | tf_op jit(solution)/shard_map/dot_general | solution.py:48
  357.7 15.7 %collective-permute-done.20 = bf16[512,1024]{1,0:T(8,128)(2,1)S(1)} collective-permute-done((bf16[512,1024]{1,0:T(8,128)(2,1)S(1)}, bf16[512,1024]{1,0:T(8,128)(2,1)S(1)}, u32[]{:S(2)}, u32[]{:S(2)}) %collective-permute-start.20) | collective-permute-done | bytes 1048608 | tf_op jit(solution)/shard_map/ppermute | solution.py:170
  373.4 2.8 multiply_reduce_fusion.2
  381.1 11.8 %collective-permute-done.21 = bf16[512,1024]{1,0:T(8,128)(2,1)S(1)} collective-permute-done((bf16[512,1024]{1,0:T(8,128)(2,1)}, bf16[512,1024]{1,0:T(8,128)(2,1)S(1)}, u32[]{:S(2)}, u32[]{:S(2)}) %collective-permute-start.21) | collective-permute-done | bytes 1048608 | tf_op jit(solution)/shard_map/ppermute | solution.py:150
  392.9 4.7 convolution_convert_fusion.3
  400.6 2.6 fusion.10
  410.5 11.3 %fusion = (f32[4,2,512]{2,1,0:T(2,128)}, f32[4,1024,512,2]{2,1,3,0:T(8,128)}) fusion(f32[4,2,512,1024]{2,3,1,0:T(8,128)S(1)} %bitcast.217, f32[4,2,512]{2,1,0:T(2,128)} %bitcast.246, bf16[512,4,2,128]{0,3,2,1:T(8,128)(2,1)} %bitcast.230, bf16[1024,4,128,1]{2,1,0,3:T(4,128)(2,1)} %bitcast.236), kind=kOutput, calls=%fused_computation.2 | convolution fusion | flops 1086320640 | bytes 35684352 | tf_op jit(solution)/shard_map/qgrd,kgd->grqk/dot_general | solution.py:113
  421.7 8.4 %fusion.2 = bf16[4,2,512,1024]{2,3,1,0:T(8,128)(2,1)S(1)} fusion(f32[4,1024,512,2]{2,1,3,0:T(8,128)} %get-tuple-element.136, f32[4,2,512,1024]{2,3,1,0:T(8,128)S(1)} %bitcast.217, f32[4,2,512]{2,1,0:T(2,128)} %get-tuple-element.135, f32[4,2,512]{2,1,0:T(2,128)} %bitcast.247), kind=kLoop, calls=%fused_computation.4 | loop fusion | flops 16777216 | bytes 41975808 | tf_op jit(solution)/shard_map/convert_element_type | solution.py:117
  435.7 3.9 copy.226
  439.6 2.8 copy.227
  442.5 4.1 multiply_subtract_fusion
  447.2 16.9 %multiply_reduce_fusion = (f32[1024,8]{1,0:T(8,128)S(1)}, f32[1024,8,128]{2,1,0:T(8,128)}) fusion(f32[1024,8,128]{2,1,0:T(8,128)S(1)} %bitcast.221, f32[128]{0:T(128)S(1)} %copy-done.93, f32[1024,8]{1,0:T(8,128)S(1)} %copy-done.26, f32[1024,8,64]{2,1,0:T(8,128)S(1)} %get-tuple-element.89, f32[1024,8,64]{2,1,0:T(8,128)S(1)} %get-tuple-element.88), kind=kLoop, calls=%fused_computation.57 | loop fusion | flops 5234688 | bytes 12648960 | tf_op jit(solution)/shard_map/reduce_sum | solution.py:43
  468.9 2.8 fusion.111
  472.8 9.9 %fusion.59 = bf16[1024,4,128]{0,2,1:T(8,128)(2,1)} fusion(f32[512,4,128]{0,2,1:T(8,128)} %fusion.100, bf16[512,4,2,128]{0,3,2,1:T(8,128)(2,1)S(1)} %bitcast.231, f32[4,2,512,1024]{2,3,1,0:T(8,128)} %get-tuple-element.129, f32[4,2,512]{2,1,0:T(2,128)S(1)} %bitcast.248), kind=kOutput, calls=%fused_computation.112 | convolution fusion | flops 1083179008 | bytes 19939328 | tf_op jit(solution)/shard_map/grqk,qgrd->kgd/dot_general | solution.py:127
  488.7 7.2 fusion.22
  502.0 4.5 fusion.60
  506.6 5.3 fusion.29
  511.8 3.2 pad_maximum_fusion.2
  516.9 6.6 convolution_convert_fusion
  523.5 4.6 reshape.393
  528.2 6.5 convolution_convert_fusion.2
  534.7 5.4 convolution_convert_fusion.1
  540.1 5.2 pad_maximum_fusion.1
  547.0 4.7 fusion.87
  558.1 8.4 %collective-permute-done.22 = bf16[512,1024]{1,0:T(8,128)(2,1)S(1)} collective-permute-done((bf16[512,1024]{1,0:T(8,128)(2,1)S(1)}, bf16[512,1024]{1,0:T(8,128)(2,1)S(1)}, u32[]{:S(2)}, u32[]{:S(2)}) %collective-permute-start.22) | collective-permute-done | bytes 1048608 | tf_op jit(solution)/shard_map/ppermute | solution.py:170
  566.5 4.9 multiply_reduce_fusion.3
  573.3 4.7 collective-permute-done.23
  579.3 2.8 add_convert_fusion.2
  582.9 4.7 collective-permute-done.26
  587.6 3.1 collective-permute-start.27
  594.1 6.5 reduce-scatter.3.cloned.1.call-done
  604.0 110.9 %reduce-scatter.5.cloned.1.call-done = bf16[64,4608]{1,0:T(8,128)(2,1)} async-done(((bf16[1024,4608]{1,0:T(8,128)(2,1)}), bf16[64,4608]{1,0:T(8,128)(2,1)}) %reduce-scatter.5.cloned.1.call-update) | async-done | bytes 589840 | tf_op jit(solution)/shard_map/reduce_scatter | solution.py:277
  (415 shorter events, 132.9 us)
Async XLA Ops:
  7.2 148.0 %copy-start.39 = (bf16[512,1024]{1,0:T(8,128)(2,1)S(1)}, bf16[512,1024]{1,0:T(8,128)(2,1)}, u32[]{:S(2)}) copy-start(bf16[512,1024]{1,0:T(8,128)(2,1)} %param.26) | copy-start | bytes 3145732
  7.2 305.1 %all-gather.2.cloned.1.call-start = ((), (), s32[]{:S(2)}) async-start(), calls=%async_computation.2 | async-start | bytes 10027008 | tf_op jit(solution)/shard_map/all_gather | solution.py:214
  8.4 11.0 %collective-permute-start.1 = (bf16[64,3072]{1,0:T(8,128)(2,1)S(1)}, bf16[64,3072]{1,0:T(8,128)(2,1)S(1)}, u32[]{:S(2)}, u32[]{:S(2)}) collective-permute-start(bf16[64,3072]{1,0:T(8,128)(2,1)S(1)} %pad_maximum_fusion.14), channel_id=1, source_target_pairs={{0,2},{2,4},{4,6},{6,8},{8,10},{10,12},{12,14},{14,16},{16,18},{18... | collective-permute-start | bytes 1179656 | tf_op jit(solution)/shard_map/ppermute | solution.py:208
  19.3 9.9 %collective-permute-start.2 = (bf16[64,3072]{1,0:T(8,128)(2,1)S(1)}, bf16[64,3072]{1,0:T(8,128)(2,1)S(1)}, u32[]{:S(2)}, u32[]{:S(2)}) collective-permute-start(bf16[64,3072]{1,0:T(8,128)(2,1)S(1)} %collective-permute-done.1), channel_id=1, source_target_pairs={{0,2},{2,4},{4,6},{6,8},{8,10},{10,12},{12,14},{14,16},{16,18},{18... | collective-permute-start | bytes 1179656 | tf_op jit(solution)/shard_map/ppermute | solution.py:208
  29.2 89.2 %copy-start.57 = (bf16[64,3072]{1,0:T(8,128)(2,1)}, bf16[64,3072]{1,0:T(8,128)(2,1)S(1)}, u32[]{:S(2)}) copy-start(bf16[64,3072]{1,0:T(8,128)(2,1)S(1)} %collective-permute-done.2) | copy-start | bytes 1179652
  29.2 9.9 %collective-permute-start.3 = (bf16[64,3072]{1,0:T(8,128)(2,1)S(1)}, bf16[64,3072]{1,0:T(8,128)(2,1)S(1)}, u32[]{:S(2)}, u32[]{:S(2)}) collective-permute-start(bf16[64,3072]{1,0:T(8,128)(2,1)S(1)} %collective-permute-done.2), channel_id=1, source_target_pairs={{0,2},{2,4},{4,6},{6,8},{8,10},{10,12},{12,14},{14,16},{16,18},{18... | collective-permute-start | bytes 1179656 | tf_op jit(solution)/shard_map/ppermute | solution.py:208
  39.1 79.3 %copy-start.59 = (bf16[64,3072]{1,0:T(8,128)(2,1)}, bf16[64,3072]{1,0:T(8,128)(2,1)S(1)}, u32[]{:S(2)}) copy-start(bf16[64,3072]{1,0:T(8,128)(2,1)S(1)} %collective-permute-done.3) | copy-start | bytes 1179652
  39.1 9.9 %collective-permute-start.4 = (bf16[64,3072]{1,0:T(8,128)(2,1)S(1)}, bf16[64,3072]{1,0:T(8,128)(2,1)S(1)}, u32[]{:S(2)}, u32[]{:S(2)}) collective-permute-start(bf16[64,3072]{1,0:T(8,128)(2,1)S(1)} %collective-permute-done.3), channel_id=1, source_target_pairs={{0,2},{2,4},{4,6},{6,8},{8,10},{10,12},{12,14},{14,16},{16,18},{18... | collective-permute-start | bytes 1179656 | tf_op jit(solution)/shard_map/ppermute | solution.py:208
  49.0 69.4 %copy-start.61 = (bf16[64,3072]{1,0:T(8,128)(2,1)}, bf16[64,3072]{1,0:T(8,128)(2,1)S(1)}, u32[]{:S(2)}) copy-start(bf16[64,3072]{1,0:T(8,128)(2,1)S(1)} %collective-permute-done.4) | copy-start | bytes 1179652
  49.0 9.9 %collective-permute-start.5 = (bf16[64,3072]{1,0:T(8,128)(2,1)S(1)}, bf16[64,3072]{1,0:T(8,128)(2,1)S(1)}, u32[]{:S(2)}, u32[]{:S(2)}) collective-permute-start(bf16[64,3072]{1,0:T(8,128)(2,1)S(1)} %collective-permute-done.4), channel_id=1, source_target_pairs={{0,2},{2,4},{4,6},{6,8},{8,10},{10,12},{12,14},{14,16},{16,18},{18... | collective-permute-start | bytes 1179656 | tf_op jit(solution)/shard_map/ppermute | solution.py:208
  58.9 81.9 %copy-start.63 = (bf16[64,3072]{1,0:T(8,128)(2,1)}, bf16[64,3072]{1,0:T(8,128)(2,1)S(1)}, u32[]{:S(2)}) copy-start(bf16[64,3072]{1,0:T(8,128)(2,1)S(1)} %collective-permute-done.5) | copy-start | bytes 1179652
  58.9 9.9 %collective-permute-start.6 = (bf16[64,3072]{1,0:T(8,128)(2,1)S(1)}, bf16[64,3072]{1,0:T(8,128)(2,1)S(1)}, u32[]{:S(2)}, u32[]{:S(2)}) collective-permute-start(bf16[64,3072]{1,0:T(8,128)(2,1)S(1)} %collective-permute-done.5), channel_id=1, source_target_pairs={{0,2},{2,4},{4,6},{6,8},{8,10},{10,12},{12,14},{14,16},{16,18},{18... | collective-permute-start | bytes 1179656 | tf_op jit(solution)/shard_map/ppermute | solution.py:208
  68.8 72.0 %copy-start.65 = (bf16[64,3072]{1,0:T(8,128)(2,1)}, bf16[64,3072]{1,0:T(8,128)(2,1)S(1)}, u32[]{:S(2)}) copy-start(bf16[64,3072]{1,0:T(8,128)(2,1)S(1)} %collective-permute-done.6) | copy-start | bytes 1179652
  68.8 9.9 %collective-permute-start.7 = (bf16[64,3072]{1,0:T(8,128)(2,1)S(1)}, bf16[64,3072]{1,0:T(8,128)(2,1)S(1)}, u32[]{:S(2)}, u32[]{:S(2)}) collective-permute-start(bf16[64,3072]{1,0:T(8,128)(2,1)S(1)} %collective-permute-done.6), channel_id=1, source_target_pairs={{0,2},{2,4},{4,6},{6,8},{8,10},{10,12},{12,14},{14,16},{16,18},{18... | collective-permute-start | bytes 1179656 | tf_op jit(solution)/shard_map/ppermute | solution.py:208
  78.7 39.8 %copy-start.67 = (bf16[64,3072]{1,0:T(8,128)(2,1)}, bf16[64,3072]{1,0:T(8,128)(2,1)S(1)}, u32[]{:S(2)}) copy-start(bf16[64,3072]{1,0:T(8,128)(2,1)S(1)} %collective-permute-done.7) | copy-start | bytes 1179652
  78.7 9.9 %collective-permute-start.8 = (bf16[64,3072]{1,0:T(8,128)(2,1)S(1)}, bf16[64,3072]{1,0:T(8,128)(2,1)S(1)}, u32[]{:S(2)}, u32[]{:S(2)}) collective-permute-start(bf16[64,3072]{1,0:T(8,128)(2,1)S(1)} %collective-permute-done.7), channel_id=1, source_target_pairs={{0,2},{2,4},{4,6},{6,8},{8,10},{10,12},{12,14},{14,16},{16,18},{18... | collective-permute-start | bytes 1179656 | tf_op jit(solution)/shard_map/ppermute | solution.py:208
  88.6 29.9 %copy-start.69 = (bf16[64,3072]{1,0:T(8,128)(2,1)}, bf16[64,3072]{1,0:T(8,128)(2,1)S(1)}, u32[]{:S(2)}) copy-start(bf16[64,3072]{1,0:T(8,128)(2,1)S(1)} %collective-permute-done.8) | copy-start | bytes 1179652
  88.6 9.9 %collective-permute-start.9 = (bf16[64,3072]{1,0:T(8,128)(2,1)S(1)}, bf16[64,3072]{1,0:T(8,128)(2,1)S(1)}, u32[]{:S(2)}, u32[]{:S(2)}) collective-permute-start(bf16[64,3072]{1,0:T(8,128)(2,1)S(1)} %collective-permute-done.8), channel_id=1, source_target_pairs={{0,2},{2,4},{4,6},{6,8},{8,10},{10,12},{12,14},{14,16},{16,18},{18... | collective-permute-start | bytes 1179656 | tf_op jit(solution)/shard_map/ppermute | solution.py:208
  98.5 20.0 %copy-start.71 = (bf16[64,3072]{1,0:T(8,128)(2,1)}, bf16[64,3072]{1,0:T(8,128)(2,1)S(1)}, u32[]{:S(2)}) copy-start(bf16[64,3072]{1,0:T(8,128)(2,1)S(1)} %collective-permute-done.9) | copy-start | bytes 1179652
  98.5 9.9 %collective-permute-start.10 = (bf16[64,3072]{1,0:T(8,128)(2,1)S(1)}, bf16[64,3072]{1,0:T(8,128)(2,1)S(1)}, u32[]{:S(2)}, u32[]{:S(2)}) collective-permute-start(bf16[64,3072]{1,0:T(8,128)(2,1)S(1)} %collective-permute-done.9), channel_id=1, source_target_pairs={{0,2},{2,4},{4,6},{6,8},{8,10},{10,12},{12,14},{14,16},{16,18},{18... | collective-permute-start | bytes 1179656 | tf_op jit(solution)/shard_map/ppermute | solution.py:208
  108.4 10.0 %collective-permute-start.11 = (bf16[64,3072]{1,0:T(8,128)(2,1)S(1)}, bf16[64,3072]{1,0:T(8,128)(2,1)}, u32[]{:S(2)}, u32[]{:S(2)}) collective-permute-start(bf16[64,3072]{1,0:T(8,128)(2,1)S(1)} %collective-permute-done.10), channel_id=1, source_target_pairs={{0,2},{2,4},{4,6},{6,8},{8,10},{10,12},{12,14},{14,16},{16,18},{18... | collective-permute-start | bytes 1179656 | tf_op jit(solution)/shard_map/ppermute | solution.py:208
  118.5 10.3 %collective-permute-start.12 = (bf16[64,3072]{1,0:T(8,128)(2,1)}, bf16[64,3072]{1,0:T(8,128)(2,1)}, u32[]{:S(2)}, u32[]{:S(2)}) collective-permute-start(bf16[64,3072]{1,0:T(8,128)(2,1)} %collective-permute-done.11), channel_id=1, source_target_pairs={{0,2},{2,4},{4,6},{6,8},{8,10},{10,12},{12,14},{14,16},{16,18},{18... | collective-permute-start | bytes 1179656 | tf_op jit(solution)/shard_map/ppermute | solution.py:208
  118.6 36.6 %collective-permute-start = (bf16[512,1024]{1,0:T(8,128)(2,1)}, bf16[512,1024]{1,0:T(8,128)(2,1)S(1)}, u32[]{:S(2)}, u32[]{:S(2)}) collective-permute-start(bf16[512,1024]{1,0:T(8,128)(2,1)} %param.26), channel_id=1, source_target_pairs={{0,1},{1,0},{2,3},{3,2},{4,5},{5,4},{6,7},{7,6},{8,9},{9,8},{10,11... | collective-permute-start | bytes 3145736 | tf_op jit(solution)/shard_map/ppermute | solution.py:150
  128.7 10.2 %collective-permute-start.13 = (bf16[64,3072]{1,0:T(8,128)(2,1)}, bf16[64,3072]{1,0:T(8,128)(2,1)}, u32[]{:S(2)}, u32[]{:S(2)}) collective-permute-start(bf16[64,3072]{1,0:T(8,128)(2,1)} %collective-permute-done.12), channel_id=1, source_target_pairs={{0,2},{2,4},{4,6},{6,8},{8,10},{10,12},{12,14},{14,16},{16,18},{18... | collective-permute-start | bytes 1179656 | tf_op jit(solution)/shard_map/ppermute | solution.py:208
  130.7 469.8 %reduce-scatter.3.cloned.1.call-start = ((), (), s32[]{:S(2)}) async-start(), calls=%async_computation.3 | async-start | bytes 6684672 | tf_op jit(solution)/shard_map/reduce_scatter | solution.py:314
  138.9 15.4 %collective-permute-start.14 = (bf16[64,3072]{1,0:T(8,128)(2,1)}, bf16[64,3072]{1,0:T(8,128)(2,1)}, u32[]{:S(2)}, u32[]{:S(2)}) collective-permute-start(bf16[64,3072]{1,0:T(8,128)(2,1)} %collective-permute-done.13), channel_id=1, source_target_pairs={{0,2},{2,4},{4,6},{6,8},{8,10},{10,12},{12,14},{14,16},{16,18},{18... | collective-permute-start | bytes 1179656 | tf_op jit(solution)/shard_map/ppermute | solution.py:208
  143.8 75.3 %copy-start.15 = (f32[1024,64]{1,0:T(8,128)}, f32[1024,64]{1,0:T(8,128)S(1)}, u32[]{:S(2)}) copy-start(f32[1024,64]{1,0:T(8,128)S(1)} %get-tuple-element.125) | copy-start | bytes 786436
  143.8 75.3 %copy-start.33 = (f32[1024,64]{1,0:T(8,128)}, f32[1024,64]{1,0:T(8,128)S(1)}, u32[]{:S(2)}) copy-start(f32[1024,64]{1,0:T(8,128)S(1)} %get-tuple-element.124) | copy-start | bytes 786436
  154.4 18.0 %collective-permute-start.15 = (bf16[64,3072]{1,0:T(8,128)(2,1)}, bf16[64,3072]{1,0:T(8,128)(2,1)}, u32[]{:S(2)}, u32[]{:S(2)}) collective-permute-start(bf16[64,3072]{1,0:T(8,128)(2,1)} %collective-permute-done.14), channel_id=1, source_target_pairs={{0,2},{2,4},{4,6},{6,8},{8,10},{10,12},{12,14},{14,16},{16,18},{18... | collective-permute-start | bytes 1179656 | tf_op jit(solution)/shard_map/ppermute | solution.py:208
  155.2 22.7 %copy-start.74 = (bf16[64,3072]{1,0:T(8,128)(2,1)S(1)}, bf16[64,3072]{1,0:T(8,128)(2,1)}, u32[]{:S(2)}) copy-start(bf16[64,3072]{1,0:T(8,128)(2,1)} %copy-done.73) | copy-start | bytes 1179652
  155.2 22.8 %copy-start.72 = (bf16[64,3072]{1,0:T(8,128)(2,1)S(1)}, bf16[64,3072]{1,0:T(8,128)(2,1)}, u32[]{:S(2)}) copy-start(bf16[64,3072]{1,0:T(8,128)(2,1)} %copy-done.71) | copy-start | bytes 1179652
  155.2 22.8 %copy-start.70 = (bf16[64,3072]{1,0:T(8,128)(2,1)S(1)}, bf16[64,3072]{1,0:T(8,128)(2,1)}, u32[]{:S(2)}) copy-start(bf16[64,3072]{1,0:T(8,128)(2,1)} %copy-done.69) | copy-start | bytes 1179652
  155.2 22.9 %copy-start.68 = (bf16[64,3072]{1,0:T(8,128)(2,1)S(1)}, bf16[64,3072]{1,0:T(8,128)(2,1)}, u32[]{:S(2)}) copy-start(bf16[64,3072]{1,0:T(8,128)(2,1)} %copy-done.67) | copy-start | bytes 1179652
  155.2 22.9 %copy-start.66 = (bf16[64,3072]{1,0:T(8,128)(2,1)S(1)}, bf16[64,3072]{1,0:T(8,128)(2,1)}, u32[]{:S(2)}) copy-start(bf16[64,3072]{1,0:T(8,128)(2,1)} %copy-done.65) | copy-start | bytes 1179652
  155.2 29.3 %copy-start.43 = (bf16[512,1024]{1,0:T(8,128)(2,1)}, bf16[512,1024]{1,0:T(8,128)(2,1)S(1)}, u32[]{:S(2)}) copy-start(bf16[512,1024]{1,0:T(8,128)(2,1)S(1)} %collective-permute-done) | copy-start | bytes 3145732
  155.7 22.4 %copy-start.64 = (bf16[64,3072]{1,0:T(8,128)(2,1)S(1)}, bf16[64,3072]{1,0:T(8,128)(2,1)}, u32[]{:S(2)}) copy-start(bf16[64,3072]{1,0:T(8,128)(2,1)} %copy-done.63) | copy-start | bytes 1179652
  155.7 28.8 %copy-start.88 = (f32[1024]{0:T(1024)}, f32[1024]{0:T(1024)S(1)}, u32[]{:S(2)}) copy-start(f32[1024]{0:T(1024)S(1)} %add_rsqrt_fusion.2) | copy-start | bytes 12292
  155.7 22.4 %copy-start.62 = (bf16[64,3072]{1,0:T(8,128)(2,1)S(1)}, bf16[64,3072]{1,0:T(8,128)(2,1)}, u32[]{:S(2)}) copy-start(bf16[64,3072]{1,0:T(8,128)(2,1)} %copy-done.61) | copy-start | bytes 1179652
  204.8 24.8 %copy-start.8 = (f32[1024,512]{1,0:T(8,128)}, f32[1024,512]{1,0:T(8,128)S(1)}, u32[]{:S(2)}) copy-start(f32[1024,512]{1,0:T(8,128)S(1)} %fusion.50) | copy-start | bytes 6291460
  229.6 149.8 %copy-start.81 = (f32[1024,4]{0,1:T(4,128)}, f32[1024,4]{0,1:T(4,128)S(1)}, u32[]{:S(2)}) copy-start(f32[1024,4]{0,1:T(4,128)S(1)} %add_rsqrt_fusion.1) | copy-start | bytes 49156
  263.5 29.8 %copy-start.102 = (bf16[4,128,2,512]{3,1,2,0:T(8,128)(2,1)}, bf16[4,128,2,512]{3,1,2,0:T(8,128)(2,1)S(1)}, u32[]{:S(2)}) copy-start(bf16[4,128,2,512]{3,1,2,0:T(8,128)(2,1)S(1)} %get-tuple-element.111) | copy-start | bytes 3145732
  263.5 32.9 %copy-start.100 = (bf16[4,128,2,512]{3,1,2,0:T(8,128)(2,1)}, bf16[4,128,2,512]{3,1,2,0:T(8,128)(2,1)S(1)}, u32[]{:S(2)}) copy-start(bf16[4,128,2,512]{3,1,2,0:T(8,128)(2,1)S(1)} %get-tuple-element.110) | copy-start | bytes 3145732
  263.5 29.8 %copy-start.40 = (bf16[512,1024]{1,0:T(8,128)(2,1)S(1)}, bf16[512,1024]{1,0:T(8,128)(2,1)}, u32[]{:S(2)}) copy-start(bf16[512,1024]{1,0:T(8,128)(2,1)} %param.26) | copy-start | bytes 3145732
  267.2 26.1 %collective-permute-start.16 = (bf16[512,1024]{1,0:T(8,128)(2,1)S(1)}, bf16[512,1024]{1,0:T(8,128)(2,1)S(1)}, u32[]{:S(2)}, u32[]{:S(2)}) collective-permute-start(bf16[512,1024]{1,0:T(8,128)(2,1)S(1)} %fusion.84), channel_id=1, source_target_pairs={{0,1},{1,0},{2,3},{3,2},{4,5},{5,4},{6,7},{7,6},{8,9},{9,8},{10,11... | collective-permute-start | bytes 3145736 | tf_op jit(solution)/shard_map/ppermute | solution.py:170
  269.2 42.0 %collective-permute-start.19 = (bf16[512,1024]{1,0:T(8,128)(2,1)S(1)}, bf16[512,1024]{1,0:T(8,128)(2,1)S(1)}, u32[]{:S(2)}, u32[]{:S(2)}) collective-permute-start(bf16[512,1024]{1,0:T(8,128)(2,1)S(1)} %copy-done.22), channel_id=1, source_target_pairs={{0,1},{1,0},{2,3},{3,2},{4,5},{5,4},{6,7},{7,6},{8,9},{9,8},{10,11... | collective-permute-start | bytes 3145736 | tf_op jit(solution)/shard_map/ppermute | solution.py:150
  296.5 79.7 %copy-start.10 = (f32[512,1024]{1,0:T(8,128)}, f32[512,1024]{1,0:T(8,128)S(1)}, u32[]{:S(2)}) copy-start(f32[512,1024]{1,0:T(8,128)S(1)} %get-tuple-element.131) | copy-start | bytes 6291460
  296.5 79.7 %copy-start.86 = (f32[512]{0:T(512)}, f32[512]{0:T(512)S(1)}, u32[]{:S(2)}) copy-start(f32[512]{0:T(512)S(1)} %add_rsqrt_fusion.3) | copy-start | bytes 6148
  297.9 32.9 %collective-permute-start.17 = (bf16[512,1024]{1,0:T(8,128)(2,1)}, bf16[512,1024]{1,0:T(8,128)(2,1)}, u32[]{:S(2)}, u32[]{:S(2)}) collective-permute-start(bf16[512,1024]{1,0:T(8,128)(2,1)} %multiply_convert_fusion.4), channel_id=1, source_target_pairs={{0,1},{1,0},{2,3},{3,2},{4,5},{5,4},{6,7},{7,6},{8,9},{9,8},{10,11... | collective-permute-start | bytes 3145736 | tf_op jit(solution)/shard_map/ppermute | solution.py:150
  350.4 23.0 %copy-start.104 = (bf16[1024,1536]{1,0:T(8,128)(2,1)}, bf16[1024,1536]{1,0:T(8,128)(2,1)S(1)}, u32[]{:S(2)}) copy-start(bf16[1024,1536]{1,0:T(8,128)(2,1)S(1)} %get-tuple-element.85) | copy-start | bytes 9437188
  354.1 19.3 %collective-permute-start.20 = (bf16[512,1024]{1,0:T(8,128)(2,1)S(1)}, bf16[512,1024]{1,0:T(8,128)(2,1)S(1)}, u32[]{:S(2)}, u32[]{:S(2)}) collective-permute-start(bf16[512,1024]{1,0:T(8,128)(2,1)S(1)} %add_convert_fusion.1), channel_id=1, source_target_pairs={{0,1},{1,0},{2,3},{3,2},{4,5},{5,4},{6,7},{7,6},{8,9},{9,8},{10,11... | collective-permute-start | bytes 3145736 | tf_op jit(solution)/shard_map/ppermute | solution.py:170
  357.7 18.5 %copy-start.23 = (bf16[512,1024]{1,0:T(8,128)(2,1)S(1)}, bf16[512,1024]{1,0:T(8,128)(2,1)}, u32[]{:S(2)}) copy-start(bf16[512,1024]{1,0:T(8,128)(2,1)} %param.39) | copy-start | bytes 3145732
  376.2 21.3 %copy-start.90 = (f32[512]{0:T(512)}, f32[512]{0:T(512)S(1)}, u32[]{:S(2)}) copy-start(f32[512]{0:T(512)S(1)} %broadcast_multiply_fusion.3) | copy-start | bytes 6148
  377.9 15.0 %collective-permute-start.21 = (bf16[512,1024]{1,0:T(8,128)(2,1)}, bf16[512,1024]{1,0:T(8,128)(2,1)S(1)}, u32[]{:S(2)}, u32[]{:S(2)}) collective-permute-start(bf16[512,1024]{1,0:T(8,128)(2,1)} %fusion.131), channel_id=1, source_target_pairs={{0,1},{1,0},{2,3},{3,2},{4,5},{5,4},{6,7},{7,6},{8,9},{9,8},{10,11... | collective-permute-start | bytes 3145736 | tf_op jit(solution)/shard_map/ppermute | solution.py:150
  380.5 18.2 %slice-start.2 = ((s8[8388608]{0:T(1024)(128)(4,1)}), s8[4194304]{0:T(1024)(128)(4,1)S(1)}, s32[]{:S(2)}) async-start(s8[8388608]{0:T(1024)(128)(4,1)} %bitcast.214), calls=%async_computation.7 | async-start | bytes 8388608
  442.4 22.5 %slice-start.8 = ((s8[8388608]{0:T(1024)(128)(4,1)}), s8[4194304]{0:T(1024)(128)(4,1)S(1)}, s32[]{:S(2)}) async-start(s8[8388608]{0:T(1024)(128)(4,1)} %bitcast.218), calls=%async_computation.13 | async-start | bytes 8388608
  515.1 199.9 %reduce-scatter.5.cloned.1.call-start = ((), (), s32[]{:S(2)}) async-start(), calls=%async_computation.4 | async-start | bytes 10027008 | tf_op jit(solution)/shard_map/reduce_scatter | solution.py:277
  551.7 14.9 %collective-permute-start.22 = (bf16[512,1024]{1,0:T(8,128)(2,1)S(1)}, bf16[512,1024]{1,0:T(8,128)(2,1)S(1)}, u32[]{:S(2)}, u32[]{:S(2)}) collective-permute-start(bf16[512,1024]{1,0:T(8,128)(2,1)S(1)} %fusion.87), channel_id=1, source_target_pairs={{0,1},{1,0},{2,3},{3,2},{4,5},{5,4},{6,7},{7,6},{8,9},{9,8},{10,11... | collective-permute-start | bytes 3145736 | tf_op jit(solution)/shard_map/ppermute | solution.py:170
  556.3 22.9 %collective-permute-start.18 = (bf16[512,1024]{1,0:T(8,128)(2,1)S(1)}, bf16[512,1024]{1,0:T(8,128)(2,1)S(1)}, u32[]{:S(2)}, u32[]{:S(2)}) collective-permute-start(bf16[512,1024]{1,0:T(8,128)(2,1)S(1)} %fusion.81), channel_id=1, source_target_pairs={{0,1},{1,0},{2,3},{3,2},{4,5},{5,4},{6,7},{7,6},{8,9},{9,8},{10,11... | collective-permute-start | bytes 3145736 | tf_op jit(solution)/shard_map/ppermute | solution.py:170
  558.1 21.1 %copy-start.11 = (f32[512,1024]{1,0:T(8,128)S(1)}, f32[512,1024]{1,0:T(8,128)}, u32[]{:S(2)}) copy-start(f32[512,1024]{1,0:T(8,128)} %copy-done.10) | copy-start | bytes 6291460
  571.5 6.4 collective-permute-start.23
  577.9 1.2 collective-permute-start.24
  579.2 3.8 collective-permute-start.25
  582.9 4.7 collective-permute-start.26
  587.6 5.4 collective-permute-start.27
  (91 other events, 520.6 us)
Sparse Core Ops, SparseCore 0:
  130.9 89.1 all-gather.1
  515.2 85.3 reduce-scatter.2
  604.7 110.2 reduce-scatter.4
